TPU v7x, 512 devices: a whole 4x8x8 slice. The times are simulated.
512 devices in a mesh: section: 8 (over x, core), expert: 64 (over y, z).
Axes of the slice: x: 4, y: 8, z: 8, core: 2. Of those that a mesh axis runs over, the one named last changes fastest.
Arguments:
- states: bfloat16 [8, 2048, 2048], P('section', 'expert'), may hold values from -24 to 24
- incoming: bfloat16 [1, 2048, 2048], P(None, 'expert'), may hold values from -24 to 24
- norm_gain: float32 [8, 2048], P('section'), may hold values from 0.5 to 2
- w_gate_up: bfloat16 [8, 64, 2048, 768], P('section', 'expert'), may hold values from -0.125 to 0.125
- w_down: bfloat16 [8, 64, 384, 2048], P('section', 'expert'), may hold values from -0.15625 to 0.15625
- routes: int32 [2, 8, 2048, 4], P(None, 'section', 'expert'), may hold values from 0 to 15, all different within a row; in each aligned block of 32 rows (0 to 31, 32 to 63, ..., all dimensions but the last counted through in order) at most 10 rows name the same one
- scores: float32 [2, 8, 2048, 4], P(None, 'section', 'expert'), may hold values from 0.05 to 1
Outputs:
- layer_out: bfloat16 [2, 8, 2048, 2048], P(None, 'section', 'expert')
Inputs may be any that keep to these rules, and one draw needn't show every extreme that they name: `routes`: in each aligned block of 32 rows (the tokens of one device at one tick and section) no expert is named by more than 10 rows, a bound that some block reaches; a row names 4 different experts.
All inputs are finite; a program needn't handle non-finite values.
Results may differ from a plain program's by a relative error of at most 0.012.
Values may be sent and summed in bfloat16 or wider, within the bound.
No kernel may reach another device: no remote copies, remote signals or barrier semaphores. Data moves between devices by JAX's collectives and lax.ppermute only.
A program may use at most 64 MiB of HBM per device.

v0:
```python
import jax
import jax.numpy as jnp
from jax import lax
from jax.sharding import PartitionSpec as P

SLICES = 4
TOPK = 4
TICKS = 2


epsilon = 1e-06


def shifted(x, axis, by):
    length = lax.axis_size(axis)
    pairs = [(i, i + by) for i in range(length) if 0 <= i + by < length]
    return lax.ppermute(x, axis, pairs)


def normalize(current, gain_values):
    values = current.astype(jnp.float32)
    mean_square = jnp.mean(values * values, axis=-1, keepdims=True)
    return (values * lax.rsqrt(mean_square + epsilon) * gain_values).astype(jnp.bfloat16)


def per_device(states, incoming, norm_gain, w_gate_up, w_down, routes, scores):
    expert_count = lax.axis_size("expert") // SLICES
    tokens = states.shape[1]
    capacity = min(tokens, max(2, 5 * tokens * TOPK // (4 * expert_count)))
    feature_width = states.shape[2]
    hidden_width = w_down.shape[2]
    section_index = lax.axis_index("section")
    gate_up_weights = w_gate_up[0, 0]
    down_weights = w_down[0, 0]
    gain_values = norm_gain[0]
    current = states[0]
    outputs = []
    for tick_index in range(TICKS):
        normed = normalize(current, gain_values)
        chosen = routes[tick_index, 0].reshape(-1)
        onehot = (chosen[:, None] == jnp.arange(expert_count, dtype=jnp.int32)[None, :]).astype(
            jnp.int32
        )
        slot_index = jnp.sum((jnp.cumsum(onehot, axis=0) - onehot) * onehot, axis=1)
        target = chosen * capacity + slot_index
        matches = jnp.arange(expert_count * capacity, dtype=jnp.int32)[:, None] == target[None, :]
        picker = jnp.sum(
            matches.reshape(expert_count * capacity, tokens, TOPK).astype(jnp.float32), axis=2
        ).astype(jnp.bfloat16)
        packed = jnp.dot(picker, normed, preferred_element_type=jnp.float32).astype(jnp.bfloat16)
        packed = packed.reshape(expert_count, 1, capacity, feature_width)
        outgoing = jnp.broadcast_to(packed, (expert_count, SLICES, capacity, feature_width))
        outgoing = outgoing.reshape(expert_count * SLICES, capacity, feature_width)
        received = lax.all_to_all(outgoing, "expert", split_axis=0, concat_axis=0, tiled=True)
        slot_count = received.shape[1]
        projected = jnp.dot(
            received.reshape(-1, feature_width), gate_up_weights, preferred_element_type=jnp.float32
        )
        hidden = (jax.nn.silu(projected[:, :hidden_width]) * projected[:, hidden_width:]).astype(
            jnp.bfloat16
        )
        serve_partial_value = jnp.dot(hidden, down_weights, preferred_element_type=jnp.float32)
        partial_value = serve_partial_value.reshape(received.shape[0], slot_count, feature_width)
        returned = lax.all_to_all(
            partial_value.astype(jnp.bfloat16), "expert", split_axis=0, concat_axis=0, tiled=True
        ).astype(partial_value.dtype)
        summed = jnp.sum(returned.reshape(expert_count, SLICES, capacity, feature_width), axis=1)
        expert_table = summed.astype(jnp.bfloat16).reshape(expert_count * capacity, feature_width)
        gathered_rows = expert_table[target]
        router_scores = scores[tick_index, 0]
        weight = router_scores / jnp.sum(router_scores, axis=-1, keepdims=True)
        branch = jnp.sum(
            weight[:, :, None]
            * gathered_rows.reshape(tokens, TOPK, feature_width).astype(jnp.float32),
            axis=1,
        )
        result = (current.astype(jnp.float32) + branch).astype(jnp.bfloat16)
        outputs.append(result)
        if tick_index + 1 < TICKS:
            passed = shifted(result, "section", 1)
            current = jnp.where(section_index == 0, incoming[tick_index], passed)
    return jnp.stack(outputs)[:, None]


def solution(mesh):
    return jax.shard_map(
        per_device,
        mesh=mesh,
        in_specs=(
            P("section", "expert", None),
            P(None, "expert", None),
            P("section", None),
            P("section", "expert", None, None),
            P("section", "expert", None, None),
            P(None, "section", "expert", None),
            P(None, "section", "expert", None),
        ),
        out_specs=P(None, "section", "expert", None),
        check_vma=False,
    )
```

profile of v0, /device:TPU:42, one launch (start us, length us, event | category | flops | bytes accessed | tf_op | source)
XLA Modules:
  0.0 621.5 jit_solution(14388220347514331353)
XLA Ops:
  5.5 2.1 convolution_convert_fusion.3
  7.7 2.2 broadcast_in_dim.10
  11.6 127.6 %all_to_all.20 = bf16[64,10,2048]{2,1,0:T(8,128)(2,1)} all-to-all(bf16[64,10,2048]{2,1,0:T(8,128)(2,1)S(1)} %bitcast.77), channel_id=1, replica_groups=mesh['section'=8,'expert'=64] {'expert'}, dimensions={0} | all-to-all | bytes 5242880 | tf_op jit(solution)/shard_map/all_to_all | solution.py:54
  139.3 5.5 reshape.202
  144.8 3.9 fusion.2
  149.8 2.0 dot_general.24
  151.8 3.2 convolution_convert_fusion.1
  155.0 3.6 copy.54
  158.6 9.0 %all-to-all-start.1 = ((bf16[64,10,2048]{2,1,0:T(8,128)(2,1)}), bf16[64,10,2048]{2,1,0:T(8,128)(2,1)}, u32[]{:S(2)}, u32[]{:S(2)}) async-start(bf16[64,10,2048]{2,1,0:T(8,128)(2,1)} %copy.54), calls=%async_computation.1 | async-start | bytes 8388608 | tf_op jit(solution)/shard_map/all_to_all | solution.py:64
  168.5 119.7 %all-to-all-done.1 = bf16[64,10,2048]{2,1,0:T(8,128)(2,1)} async-done(((bf16[64,10,2048]{2,1,0:T(8,128)(2,1)}), bf16[64,10,2048]{2,1,0:T(8,128)(2,1)}, u32[]{:S(2)}, u32[]{:S(2)}) %all-to-all-start.1) | async-done | bytes 2621472 | tf_op jit(solution)/shard_map/all_to_all | solution.py:64
  288.1 4.3 bitcast_reduce_fusion.1
  292.4 2.1 convert_element_type.104
  294.6 3.4 gather_fusion
  298.0 2.4 reshape.210
  300.4 2.0 multiply_reduce_fusion.1
  303.1 1.9 collective-permute-start
  305.7 3.9 collective-permute-done
  311.4 1.9 convolution_convert_fusion.2
  313.4 2.2 broadcast_in_dim.12
  317.3 123.1 %all_to_all.21 = bf16[64,10,2048]{2,1,0:T(8,128)(2,1)} all-to-all(bf16[64,10,2048]{2,1,0:T(8,128)(2,1)S(1)} %bitcast.78), channel_id=1, replica_groups=mesh['section'=8,'expert'=64] {'expert'}, dimensions={0} | all-to-all | bytes 5242880 | tf_op jit(solution)/shard_map/all_to_all | solution.py:54
  440.4 5.5 reshape.206
  445.9 3.9 fusion
  450.9 2.0 dot_general.28
  452.9 3.2 convolution_convert_fusion
  456.1 3.6 copy.62
  459.7 12.3 %all-to-all-start.3 = ((bf16[64,10,2048]{2,1,0:T(8,128)(2,1)}), bf16[64,10,2048]{2,1,0:T(8,128)(2,1)}, u32[]{:S(2)}, u32[]{:S(2)}) async-start(bf16[64,10,2048]{2,1,0:T(8,128)(2,1)} %copy.62), calls=%async_computation.3 | async-start | bytes 8388608 | tf_op jit(solution)/shard_map/all_to_all | solution.py:64
  476.0 130.4 %all-to-all-done.3 = bf16[64,10,2048]{2,1,0:T(8,128)(2,1)} async-done(((bf16[64,10,2048]{2,1,0:T(8,128)(2,1)}), bf16[64,10,2048]{2,1,0:T(8,128)(2,1)}, u32[]{:S(2)}, u32[]{:S(2)}) %all-to-all-start.3) | async-done | bytes 2621472 | tf_op jit(solution)/shard_map/all_to_all | solution.py:64
  606.3 4.3 bitcast_reduce_fusion
  610.6 2.1 convert_element_type.118
  612.8 3.6 gather_fusion.1
  616.3 2.4 reshape.211
  618.7 2.0 multiply_reduce_fusion
  (56 shorter events, 19.9 us)
Async XLA Ops:
  0.0 144.8 %copy-start = (bf16[1,1,2048,768]{3,2,1,0:T(8,128)(2,1)S(1)}, bf16[1,1,2048,768]{3,2,1,0:T(8,128)(2,1)}, u32[]{:S(2)}) copy-start(bf16[1,1,2048,768]{3,2,1,0:T(8,128)(2,1)} %param.10) | copy-start | bytes 9437188
  4.0 7.6 %copy-start.6 = (s32[128]{0:T(128)}, s32[128]{0:T(128)S(1)}, u32[]{:S(2)}) copy-start(s32[128]{0:T(128)S(1)} %select_reduce_fusion) | copy-start | bytes 1540
  158.6 9.2 %copy-start.5 = (f32[2,1,32,4]{2,3,1,0:T(4,128)S(1)}, f32[2,1,32,4]{2,3,1,0:T(4,128)}, u32[]{:S(2)}) copy-start(f32[2,1,32,4]{2,3,1,0:T(4,128)} %param.13) | copy-start | bytes 3076
  158.6 129.6 %all-to-all-start.1 = ((bf16[64,10,2048]{2,1,0:T(8,128)(2,1)}), bf16[64,10,2048]{2,1,0:T(8,128)(2,1)}, u32[]{:S(2)}, u32[]{:S(2)}) async-start(bf16[64,10,2048]{2,1,0:T(8,128)(2,1)} %copy.54), calls=%async_computation.1 | async-start | bytes 8388608 | tf_op jit(solution)/shard_map/all_to_all | solution.py:64
  298.0 4.4 copy-start.1
  303.1 6.6 %collective-permute-start = (bf16[32,2048]{1,0:T(8,128)(2,1)}, bf16[32,2048]{1,0:T(8,128)(2,1)}, u32[]{:S(2)}, u32[]{:S(2)}) collective-permute-start(bf16[32,2048]{1,0:T(8,128)(2,1)} %fusion.16), channel_id=1, source_target_pairs={{0,64},{64,128},{128,192},{192,256},{256,320},{320,384},{384,448},... | collective-permute-start | bytes 393224 | tf_op jit(solution)/shard_map/ppermute | solution.py:17
  310.8 0.7 copy-start.2
  459.7 146.7 %all-to-all-start.3 = ((bf16[64,10,2048]{2,1,0:T(8,128)(2,1)}), bf16[64,10,2048]{2,1,0:T(8,128)(2,1)}, u32[]{:S(2)}, u32[]{:S(2)}) async-start(bf16[64,10,2048]{2,1,0:T(8,128)(2,1)} %copy.62), calls=%async_computation.3 | async-start | bytes 8388608 | tf_op jit(solution)/shard_map/all_to_all | solution.py:64
  616.3 4.4 copy-start.3
  616.3 4.4 copy-start.4
where the time goes:
time: 623 us; the launch traced here: 621 us
  waiting for transfers between devices  254 us (41%)
  blocking collectives  251 us (40%)
  local copies, waits for them, and re-layouts  49.9 us (8%)
  other arithmetic  25.2 us (4%)
  starting transfers between devices  23.2 us (4%)
  matrix products  18.3 us (3%)
    all_to_all x2, blocking collectives, per_device(): lax.all_to_all(outgoing, 'expert', split_axis=0, concat_axis=0, tiled=True)  251 us
    all_to_all x2, waiting for transfers between devices, per_device(): lax.all_to_all(partial_value.astype(jnp.bfloat16), 'expert', split_axis=0...  250 us
    all_to_all x2, starting transfers between devices, per_device(): lax.all_to_all(partial_value.astype(jnp.bfloat16), 'expert', split_axis=0...  21.3 us
  transfers between devices with their start and end apart: 3, of which 3 were waited for; matrix products, arithmetic and copies ran while one was open for 1% of the time, Pallas kernels for 0%

commit v1 on v0

v1 whole, which is shorter than its diff:
```python
import jax
import jax.numpy as jnp
from jax import lax
from jax.sharding import PartitionSpec as P

SLICES = 4
TOPK = 4
TICKS = 2
LANES = 128
ROWS = 8
SHARE = 2


epsilon = 1e-06


def shifted(x, axis, by):
    length = lax.axis_size(axis)
    pairs = [(i, i + by) for i in range(length) if 0 <= i + by < length]
    return lax.ppermute(x, axis, pairs)


def normalize(current, gain_values):
    values = current.astype(jnp.float32)
    mean_square = jnp.mean(values * values, axis=-1, keepdims=True)
    return (values * lax.rsqrt(mean_square + epsilon) * gain_values).astype(jnp.bfloat16)


def to_tiles(rows, groups):
    r = rows.shape[0] // groups
    blocks = rows.shape[1] // LANES
    return rows.reshape(groups, r, blocks, LANES).transpose(0, 2, 1, 3).reshape(groups, blocks * r, LANES)


def from_tiles(tiles, r):
    groups, _, _ = tiles.shape
    blocks = tiles.shape[1] // r
    return tiles.reshape(groups, blocks, r, LANES).transpose(0, 2, 1, 3).reshape(groups * r, blocks * LANES)


def slots_of(chosen, expert_count):
    onehot = (chosen[:, None] == jnp.arange(expert_count, dtype=jnp.int32)[None, :]).astype(jnp.int32)
    return jnp.sum((jnp.cumsum(onehot, axis=0) - onehot) * onehot, axis=1)


def exchange(x):
    length = lax.axis_size("expert")
    groups = [list(range(first, length, SHARE)) for first in range(SHARE)]
    return lax.all_to_all(x, "expert", split_axis=0, concat_axis=0, tiled=True, axis_index_groups=groups)


def swapped(x):
    length = lax.axis_size("expert")
    return lax.ppermute(x, "expert", [(i, i ^ 1) for i in range(length)])


def per_device(states, incoming, norm_gain, w_gate_up, w_down, routes, scores):
    group = lax.axis_size("expert") // SHARE
    copies = SLICES // SHARE
    expert_count = group // copies
    tokens = states.shape[1]
    capacity = min(tokens, max(2, 5 * tokens * TOPK // (4 * expert_count)))
    parts = []
    low = 0
    while low < capacity:
        high = min(low + ROWS, capacity)
        parts.append((low, high))
        low = high
    hidden_width = w_down.shape[2]
    section_index = lax.axis_index("section")
    gate_up_weights = [w_gate_up[0, 0], swapped(w_gate_up[0, 0])]
    down_weights = [w_down[0, 0], swapped(w_down[0, 0])]
    gain_values = norm_gain[0]
    plans = []
    for tick_index in range(TICKS):
        chosen = routes[tick_index, 0].reshape(-1)
        slot = slots_of(chosen, expert_count)
        router_scores = scores[tick_index, 0]
        weight = (router_scores / jnp.sum(router_scores, axis=-1, keepdims=True)).reshape(-1)
        plan = []
        for low, high in parts:
            size = high - low
            inside = (slot >= low) & (slot < high)
            target = jnp.where(inside, chosen * size + slot - low, -1)
            matches = jnp.arange(expert_count * size, dtype=jnp.int32)[:, None] == target[None, :]
            matches = matches.reshape(expert_count * size, tokens, TOPK)
            picker = jnp.any(matches, axis=2).astype(jnp.bfloat16)
            weights = jnp.sum(jnp.where(matches, weight.reshape(1, tokens, TOPK), 0.0), axis=2)
            upper = weights.astype(jnp.bfloat16)
            lower = (weights - upper.astype(jnp.float32)).astype(jnp.bfloat16)
            plan.append((picker, upper, lower))
        plans.append(plan)
    current = states[0]
    outputs = []
    for tick_index in range(TICKS):
        plan = plans[tick_index]
        normed = normalize(current, gain_values)
        sent = []
        for (low, high), (picker, _, _) in zip(parts, plan):
            packed = jnp.dot(picker, normed, preferred_element_type=jnp.float32).astype(jnp.bfloat16)
            sent.append(to_tiles(packed, expert_count))
        received = exchange(jnp.repeat(jnp.concatenate(sent, axis=1), copies, axis=0))
        at = [sum(p.shape[1] for p in sent[:i]) for i in range(len(sent) + 1)]
        rows_in = [from_tiles(received[:, at[i]:at[i + 1]], high - low) for i, (low, high) in enumerate(parts)]
        rows_in = jnp.concatenate(rows_in, axis=0)
        partial_value = 0.0
        for gate_up, down in zip(gate_up_weights, down_weights):
            projected = jnp.dot(rows_in, gate_up, preferred_element_type=jnp.float32)
            hidden = (jax.nn.silu(projected[:, :hidden_width]) * projected[:, hidden_width:]).astype(jnp.bfloat16)
            partial_value = partial_value + jnp.dot(hidden, down, preferred_element_type=jnp.float32)
        partial_value = partial_value.astype(jnp.bfloat16)
        split = [partial_value[group * low:group * high] for low, high in parts]
        back = exchange(jnp.concatenate([to_tiles(piece, group) for piece in split], axis=1))
        returned = [back[:, at[i]:at[i + 1]] for i in range(len(sent))]
        branch = 0.0
        for (low, high), piece, (_, upper, lower) in zip(parts, returned, plan):
            summed = jnp.sum(piece.reshape(expert_count, copies, piece.shape[1], LANES).astype(jnp.float32), axis=1)
            table = from_tiles(summed.astype(jnp.bfloat16), high - low)
            contract = (((0,), (0,)), ((), ()))
            branch = branch + lax.dot_general(upper, table, contract, preferred_element_type=jnp.float32)
            branch = branch + lax.dot_general(lower, table, contract, preferred_element_type=jnp.float32)
        result = (current.astype(jnp.float32) + branch).astype(jnp.bfloat16)
        outputs.append(result)
        if tick_index + 1 < TICKS:
            passed = shifted(result, "section", 1)
            current = jnp.where(section_index == 0, incoming[tick_index], passed)
    return jnp.stack(outputs)[:, None]


def solution(mesh):
    return jax.shard_map(
        per_device,
        mesh=mesh,
        in_specs=(
            P("section", "expert", None),
            P(None, "expert", None),
            P("section", None),
            P("section", "expert", None, None),
            P("section", "expert", None, None),
            P(None, "section", "expert", None),
            P(None, "section", "expert", None),
        ),
        out_specs=P(None, "section", "expert", None),
        check_vma=False,
    )
```

time: 623 us -> 309 us (0.50)
  the two profiles are of different devices: /device:TPU:42 before, /device:TPU:56 now
where the time goes in v1:
time: 309 us
  waiting for transfers between devices  193 us (62%)
  blocking collectives  43.1 us (14%)
  starting transfers between devices  40.7 us (13%)
  matrix products  15.9 us (5%)
  local copies, waits for them, and re-layouts  8.88 us (3%)
  other arithmetic  6.82 us (2%)
    all_to_all x3, waiting for transfers between devices, exchange(): lax.all_to_all(x, 'expert', split_axis=0, concat_axis=0, tiled=True, axis...  100 us
    ppermute x2, waiting for transfers between devices, swapped(): return lax.ppermute(x, 'expert', [(i, i ^ 1) for i in range(length)])  91.3 us
    all_to_all x1, blocking collectives, exchange(): lax.all_to_all(x, 'expert', split_axis=0, concat_axis=0, tiled=True, axis...  43.1 us
    all_to_all x3, starting transfers between devices, exchange(): lax.all_to_all(x, 'expert', split_axis=0, concat_axis=0, tiled=True, axis...  33.6 us
    dot_general x4, matrix products, per_device(): projected = jnp.dot(rows_in, gate_up, preferred_element_type=jnp.float32)  8.55 us
  transfers between devices with their start and end apart: 6, of which 6 were waited for; matrix products, arithmetic and copies ran while one was open for 2% of the time, Pallas kernels for 0%

profile of v1, /device:TPU:56, one launch (start us, length us, event | category | flops | bytes accessed | tf_op | source)
XLA Modules:
  0.0 308.7 jit_solution(8211307844932658927)
XLA Ops:
  0.0 0.7 multiply_bitcast_fusion.1
  1.8 1.0 fusion.28
  2.8 1.1 fusion.13
  4.3 0.4 fusion.11
  4.8 1.3 broadcast_in_dim.69
  6.0 15.6 %all-to-all-start = ((bf16[32,160,128]{2,1,0:T(8,128)(2,1)}), bf16[32,160,128]{2,1,0:T(8,128)(2,1)S(1)}, u32[]{:S(2)}, u32[]{:S(2)}) async-start(bf16[32,160,128]{2,1,0:T(8,128)(2,1)} %bitcast.11), calls=%async_computation | async-start | bytes 2621440 | tf_op jit(solution)/shard_map/all_to_all | solution.py:49
  21.6 3.4 %collective-permute-start = (bf16[2048,768]{1,0:T(8,128)(2,1)}, bf16[2048,768]{1,0:T(8,128)(2,1)}, u32[]{:S(2)}, u32[]{:S(2)}) collective-permute-start(bf16[2048,768]{1,0:T(8,128)(2,1)} %bitcast.214), channel_id=1, source_target_pairs={{0,1},{1,0},{2,3},{3,2},{4,5},{5,4},{6,7},{7,6},{8,9},{9,8},{10,11... | collective-permute-start | bytes 9437192 | tf_op jit(solution)/shard_map/ppermute | solution.py:54
  25.0 2.5 collective-permute-start.1
  27.5 27.5 %all-to-all-done = bf16[32,160,128]{2,1,0:T(8,128)(2,1)S(1)} async-done(((bf16[32,160,128]{2,1,0:T(8,128)(2,1)}), bf16[32,160,128]{2,1,0:T(8,128)(2,1)S(1)}, u32[]{:S(2)}, u32[]{:S(2)}) %all-to-all-start) | async-done | bytes 1310752 | tf_op jit(solution)/shard_map/all_to_all | solution.py:49
  56.0 1.4 copy-done.4
  57.4 1.2 fusion.75
  58.8 0.9 fusion.31
  59.7 61.6 %collective-permute-done = bf16[2048,768]{1,0:T(8,128)(2,1)} collective-permute-done((bf16[2048,768]{1,0:T(8,128)(2,1)}, bf16[2048,768]{1,0:T(8,128)(2,1)}, u32[]{:S(2)}, u32[]{:S(2)}) %collective-permute-start) | collective-permute-done | bytes 3145760 | tf_op jit(solution)/shard_map/ppermute | solution.py:54
  121.3 3.1 %fusion.81 = f32[320,768]{1,0:T(8,128)S(1)} fusion(bf16[320,2048]{1,0:T(8,128)(2,1)S(1)} %bitcast_dynamic-update-slice_fusion.3, bf16[2048,768]{1,0:T(8,128)(2,1)} %collective-permute-done), kind=kOutput, calls=%fused_computation.141 | convolution fusion | flops 1006632960 | bytes 5439488 | tf_op jit(solution)/shard_map/dot_general | solution.py:108
  124.4 29.7 %collective-permute-done.1 = bf16[384,2048]{1,0:T(8,128)(2,1)S(1)} collective-permute-done((bf16[384,2048]{1,0:T(8,128)(2,1)}, bf16[384,2048]{1,0:T(8,128)(2,1)S(1)}, u32[]{:S(2)}, u32[]{:S(2)}) %collective-permute-start.1) | collective-permute-done | bytes 1572896 | tf_op jit(solution)/shard_map/ppermute | solution.py:54
  154.1 0.9 fusion
  155.4 1.2 pad_maximum_fusion
  156.6 10.3 %all-to-all-start.1 = ((bf16[32,160,128]{2,1,0:T(8,128)(2,1)}), bf16[32,160,128]{2,1,0:T(8,128)(2,1)S(1)}, u32[]{:S(2)}, u32[]{:S(2)}) async-start(bf16[32,160,128]{2,1,0:T(8,128)(2,1)} %pad_maximum_fusion), calls=%async_computation.1 | async-start | bytes 2621440 | tf_op jit(solution)/shard_map/all_to_all | solution.py:49
  168.0 32.2 %all-to-all-done.1 = bf16[32,160,128]{2,1,0:T(8,128)(2,1)S(1)} async-done(((bf16[32,160,128]{2,1,0:T(8,128)(2,1)}), bf16[32,160,128]{2,1,0:T(8,128)(2,1)S(1)}, u32[]{:S(2)}, u32[]{:S(2)}) %all-to-all-start.1) | async-done | bytes 1310752 | tf_op jit(solution)/shard_map/all_to_all | solution.py:49
  201.5 1.3 collective-permute-start.2
  203.0 0.8 collective-permute-done.2
  203.9 0.4 fusion.12
  204.9 43.1 %all_to_all.20 = bf16[32,160,128]{2,1,0:T(8,128)(2,1)S(1)} all-to-all(bf16[32,160,128]{2,1,0:T(8,128)(2,1)S(1)} %bitcast.188), channel_id=1, replica_groups={{0,2,4,6,8,10,12,14,16,18,20,22,24,26,28,30,32,34,36,38,40,42,44,46,48,..., dimensions={0} | all-to-all | bytes 2621440 | tf_op jit(solution)/shard_map/all_to_all | solution.py:49
  249.1 1.3 copy-done.5
  250.3 1.2 fusion.73
  251.7 0.9 fusion.34
  252.6 3.1 %fusion.82 = f32[320,768]{1,0:T(8,128)S(1)} fusion(bf16[320,2048]{1,0:T(8,128)(2,1)S(1)} %bitcast_dynamic-update-slice_fusion.2, bf16[2048,768]{1,0:T(8,128)(2,1)} %collective-permute-done), kind=kOutput, calls=%fused_computation.142 | convolution fusion | flops 1006632960 | bytes 5439488 | tf_op jit(solution)/shard_map/dot_general | solution.py:108
  255.7 0.9 fusion.1
  257.0 1.2 pad_maximum_fusion.1
  258.1 7.7 %all-to-all-start.3 = ((bf16[32,160,128]{2,1,0:T(8,128)(2,1)}), bf16[32,160,128]{2,1,0:T(8,128)(2,1)S(1)}, u32[]{:S(2)}, u32[]{:S(2)}) async-start(bf16[32,160,128]{2,1,0:T(8,128)(2,1)} %pad_maximum_fusion.1), calls=%async_computation.3 | async-start | bytes 2621440 | tf_op jit(solution)/shard_map/all_to_all | solution.py:49
  266.0 40.7 %all-to-all-done.3 = bf16[32,160,128]{2,1,0:T(8,128)(2,1)S(1)} async-done(((bf16[32,160,128]{2,1,0:T(8,128)(2,1)}), bf16[32,160,128]{2,1,0:T(8,128)(2,1)S(1)}, u32[]{:S(2)}, u32[]{:S(2)}) %all-to-all-start.3) | async-done | bytes 1310752 | tf_op jit(solution)/shard_map/all_to_all | solution.py:49
  307.9 0.7 maximum_bitcast_fusion
  (99 shorter events, 8.8 us)
Async XLA Ops:
  0.0 4.3 %copy-start = (bf16[1,32,2048]{2,1,0:T(8,128)(2,1)S(1)}, bf16[1,32,2048]{2,1,0:T(8,128)(2,1)}, u32[]{:S(2)}) copy-start(bf16[1,32,2048]{2,1,0:T(8,128)(2,1)} %param.7) | copy-start | bytes 393220
  0.0 4.3 %copy-start.1 = (f32[1,2048]{1,0:T(1,128)S(1)}, f32[1,2048]{1,0:T(1,128)}, u32[]{:S(2)}) copy-start(f32[1,2048]{1,0:T(1,128)} %param.9) | copy-start | bytes 24580
  6.0 49.0 %all-to-all-start = ((bf16[32,160,128]{2,1,0:T(8,128)(2,1)}), bf16[32,160,128]{2,1,0:T(8,128)(2,1)S(1)}, u32[]{:S(2)}, u32[]{:S(2)}) async-start(bf16[32,160,128]{2,1,0:T(8,128)(2,1)} %bitcast.11), calls=%async_computation | async-start | bytes 2621440 | tf_op jit(solution)/shard_map/all_to_all | solution.py:49
  21.6 99.7 %collective-permute-start = (bf16[2048,768]{1,0:T(8,128)(2,1)}, bf16[2048,768]{1,0:T(8,128)(2,1)}, u32[]{:S(2)}, u32[]{:S(2)}) collective-permute-start(bf16[2048,768]{1,0:T(8,128)(2,1)} %bitcast.214), channel_id=1, source_target_pairs={{0,1},{1,0},{2,3},{3,2},{4,5},{5,4},{6,7},{7,6},{8,9},{9,8},{10,11... | collective-permute-start | bytes 9437192 | tf_op jit(solution)/shard_map/ppermute | solution.py:54
  25.0 129.1 %collective-permute-start.1 = (bf16[384,2048]{1,0:T(8,128)(2,1)}, bf16[384,2048]{1,0:T(8,128)(2,1)S(1)}, u32[]{:S(2)}, u32[]{:S(2)}) collective-permute-start(bf16[384,2048]{1,0:T(8,128)(2,1)} %bitcast.215), channel_id=1, source_target_pairs={{0,1},{1,0},{2,3},{3,2},{4,5},{5,4},{6,7},{7,6},{8,9},{9,8},{10,11... | collective-permute-start | bytes 4718600 | tf_op jit(solution)/shard_map/ppermute | solution.py:54
  55.5 1.9 copy-start.4
  57.4 1.4 copy-start.6
  156.6 11.3 %copy-start.3 = (f32[2,1,32,4]{2,3,1,0:T(4,128)S(1)}, f32[2,1,32,4]{2,3,1,0:T(4,128)}, u32[]{:S(2)}) copy-start(f32[2,1,32,4]{2,3,1,0:T(4,128)} %param.13) | copy-start | bytes 3076
  156.6 43.7 %all-to-all-start.1 = ((bf16[32,160,128]{2,1,0:T(8,128)(2,1)}), bf16[32,160,128]{2,1,0:T(8,128)(2,1)S(1)}, u32[]{:S(2)}, u32[]{:S(2)}) async-start(bf16[32,160,128]{2,1,0:T(8,128)(2,1)} %pad_maximum_fusion), calls=%async_computation.1 | async-start | bytes 2621440 | tf_op jit(solution)/shard_map/all_to_all | solution.py:49
  201.0 2.7 copy-start.2
  201.5 2.3 collective-permute-start.2
  248.4 1.9 copy-start.5
  250.3 1.4 copy-start.7
  258.1 48.6 %all-to-all-start.3 = ((bf16[32,160,128]{2,1,0:T(8,128)(2,1)}), bf16[32,160,128]{2,1,0:T(8,128)(2,1)S(1)}, u32[]{:S(2)}, u32[]{:S(2)}) async-start(bf16[32,160,128]{2,1,0:T(8,128)(2,1)} %pad_maximum_fusion.1), calls=%async_computation.3 | async-start | bytes 2621440 | tf_op jit(solution)/shard_map/all_to_all | solution.py:49

commit v2 on v1

--- a/solution.py
+++ b/solution.py
@@ -8,6 +8,7 @@
 TICKS = 2
 LANES = 128
 ROWS = 8
+COLUMNS = 8
 SHARE = 2
 
 
@@ -49,9 +50,63 @@
     return lax.all_to_all(x, "expert", split_axis=0, concat_axis=0, tiled=True, axis_index_groups=groups)
 
 
+def same_side(x):
+    length = lax.axis_size("expert")
+    pieces = [x]
+    for by in range(SHARE, COLUMNS, SHARE):
+        pairs = [(i, i // COLUMNS * COLUMNS + (i + by) % COLUMNS) for i in range(length)]
+        pieces.append(lax.ppermute(x, "expert", pairs))
+    return jnp.stack(pieces)
+
+
+def exchange_rows(x):
+    length = lax.axis_size("expert")
+    groups = [list(range(first, length, COLUMNS)) for first in range(COLUMNS)]
+    return lax.all_to_all(x, "expert", split_axis=0, concat_axis=0, tiled=True, axis_index_groups=groups)
+
+
 def swapped(x):
     length = lax.axis_size("expert")
     return lax.ppermute(x, "expert", [(i, i ^ 1) for i in range(length)])
+
+
+def first_dispatch(normed, chosen, parts, column, expert_count, swapped_first):
+    tokens, width = normed.shape
+    rows_of_chips = lax.axis_size("expert") // COLUMNS
+    halves = expert_count // rows_of_chips
+    sources = COLUMNS // SHARE
+    slot = slots_of(chosen.reshape(-1), expert_count).reshape(tokens, TOPK)
+    named = chosen[:, :, None] == jnp.arange(expert_count, dtype=jnp.int32)[None, None, :]
+    slot_at = jnp.sum(jnp.where(named, slot[:, :, None] + 1, 0), axis=1)
+    slot_at = jnp.pad(slot_at, ((0, 0), (0, LANES - expert_count))).astype(jnp.bfloat16)
+    everyone = same_side(jnp.concatenate([normed, slot_at], axis=1))
+    mine = column // SHARE
+    position = (mine - jnp.arange(sources, dtype=jnp.int32)) % sources
+    origin = jnp.arange(sources, dtype=jnp.int32)[:, None] == position[None, :]
+    slots = everyone[:, :, width:width + expert_count].astype(jnp.int32) - 1
+    slots = slots.reshape(sources, tokens, rows_of_chips, halves)
+    half = column // (COLUMNS // halves)
+    slots = jnp.sum(jnp.where(jnp.arange(halves, dtype=jnp.int32) == half, slots, 0), axis=3)
+    pieces = []
+    for low, high in parts:
+        place = jnp.arange(low, high, dtype=jnp.int32)
+        match = slots.transpose(2, 0, 1)[:, None, None, :, :] == place[None, None, :, None, None]
+        match = match & origin[None, :, None, :, None]
+        pieces.append(match.reshape(rows_of_chips, sources * (high - low), sources * tokens))
+    picker = jnp.concatenate(pieces, axis=1).astype(jnp.bfloat16)
+    count = picker.shape[1]
+    flat = everyone[:, :, :width].reshape(sources * tokens, width)
+    packed = jnp.dot(picker.reshape(rows_of_chips * count, sources * tokens), flat, preferred_element_type=jnp.float32)
+    packed = packed.astype(jnp.bfloat16).reshape(rows_of_chips, count, width)
+    packed, _ = lax.optimization_barrier((packed, swapped_first))
+    received = exchange_rows(packed)
+    rows_in = []
+    first = 0
+    for low, high in parts:
+        size = sources * (high - low)
+        rows_in.append(received[:, first:first + size].reshape(rows_of_chips * size, width))
+        first += size
+    return jnp.concatenate(rows_in, axis=0)
 
 
 def per_device(states, incoming, norm_gain, w_gate_up, w_down, routes, scores):
@@ -67,6 +122,7 @@
         parts.append((low, high))
         low = high
     hidden_width = w_down.shape[2]
+    column = lax.axis_index("expert") % COLUMNS
     section_index = lax.axis_index("section")
     gate_up_weights = [w_gate_up[0, 0], swapped(w_gate_up[0, 0])]
     down_weights = [w_down[0, 0], swapped(w_down[0, 0])]
@@ -95,14 +151,19 @@
     for tick_index in range(TICKS):
         plan = plans[tick_index]
         normed = normalize(current, gain_values)
-        sent = []
-        for (low, high), (picker, _, _) in zip(parts, plan):
-            packed = jnp.dot(picker, normed, preferred_element_type=jnp.float32).astype(jnp.bfloat16)
-            sent.append(to_tiles(packed, expert_count))
-        received = exchange(jnp.repeat(jnp.concatenate(sent, axis=1), copies, axis=0))
-        at = [sum(p.shape[1] for p in sent[:i]) for i in range(len(sent) + 1)]
-        rows_in = [from_tiles(received[:, at[i]:at[i + 1]], high - low) for i, (low, high) in enumerate(parts)]
-        rows_in = jnp.concatenate(rows_in, axis=0)
+        at = [0]
+        for low, high in parts:
+            at.append(at[-1] + (high - low) * normed.shape[1] // LANES)
+        if tick_index == 0:
+            rows_in = first_dispatch(normed, routes[0, 0], parts, column, expert_count, gate_up_weights[1])
+        else:
+            sent = []
+            for (low, high), (picker, _, _) in zip(parts, plan):
+                packed = jnp.dot(picker, normed, preferred_element_type=jnp.float32).astype(jnp.bfloat16)
+                sent.append(to_tiles(packed, expert_count))
+            received = exchange(jnp.repeat(jnp.concatenate(sent, axis=1), copies, axis=0))
+            rows_in = [from_tiles(received[:, at[i]:at[i + 1]], high - low) for i, (low, high) in enumerate(parts)]
+            rows_in = jnp.concatenate(rows_in, axis=0)
         partial_value = 0.0
         for gate_up, down in zip(gate_up_weights, down_weights):
             projected = jnp.dot(rows_in, gate_up, preferred_element_type=jnp.float32)
@@ -111,7 +172,7 @@
         partial_value = partial_value.astype(jnp.bfloat16)
         split = [partial_value[group * low:group * high] for low, high in parts]
         back = exchange(jnp.concatenate([to_tiles(piece, group) for piece in split], axis=1))
-        returned = [back[:, at[i]:at[i + 1]] for i in range(len(sent))]
+        returned = [back[:, at[i]:at[i + 1]] for i in range(len(parts))]
         branch = 0.0
         for (low, high), piece, (_, upper, lower) in zip(parts, returned, plan):
             summed = jnp.sum(piece.reshape(expert_count, copies, piece.shape[1], LANES).astype(jnp.float32), axis=1)

time: 309 us -> 289 us (0.935)
  waiting for transfers between devices: 193 us -> 161 us
  starting transfers between devices: 40.7 us -> 51 us
    ppermute x2, waiting for transfers between devices: 91.3 us -> 0.39 us  [swapped(): return lax.ppermute(x, 'expert', [(i, i ^ 1) for i in range(length)])]
    ppermute x0 -> x3, waiting for transfers between devices: none -> 65.8 us  [same_side(): pieces.append(lax.ppermute(x, 'expert', pairs))]
    all_to_all x3 -> x2, waiting for transfers between devices: 100 us -> 69.2 us  [exchange(): lax.all_to_all(x, 'expert', split_axis=0, concat_axis=0, tiled=True, axis...]
    all_to_all x0 -> x1, waiting for transfers between devices: none -> 25.1 us  [exchange_rows(): lax.all_to_all(x, 'expert', split_axis=0, concat_axis=0, tiled=True, axis...]
    ppermute x0 -> x3, starting transfers between devices: none -> 18 us  [same_side(): pieces.append(lax.ppermute(x, 'expert', pairs))]
    all_to_all x3 -> x2, starting transfers between devices: 33.6 us -> 18.7 us  [exchange(): lax.all_to_all(x, 'expert', split_axis=0, concat_axis=0, tiled=True, axis...]
    all_to_all x0 -> x1, starting transfers between devices: none -> 6.87 us  [exchange_rows(): lax.all_to_all(x, 'expert', split_axis=0, concat_axis=0, tiled=True, axis...]
  transfers between devices with their start and end apart: 6 -> 9, of which waited for: 6 -> 7; matrix products, arithmetic and copies ran while one was open for 2% -> 5% of each run, Pallas kernels for 0% -> 0%
where the time goes in v2:
time: 289 us; the launch traced here: 288 us
  waiting for transfers between devices  161 us (56%)
  starting transfers between devices  51 us (18%)
  blocking collectives  42.9 us (15%)
  matrix products  17.9 us (6%)
  other arithmetic  8.06 us (3%)
  local copies, waits for them, and re-layouts  6.3 us (2%)
    all_to_all x2, waiting for transfers between devices, exchange(): lax.all_to_all(x, 'expert', split_axis=0, concat_axis=0, tiled=True, axis...  69.2 us
    ppermute x3, waiting for transfers between devices, same_side(): pieces.append(lax.ppermute(x, 'expert', pairs))  65.8 us
    all_to_all x1, blocking collectives, exchange(): lax.all_to_all(x, 'expert', split_axis=0, concat_axis=0, tiled=True, axis...  42.9 us
    all_to_all x1, waiting for transfers between devices, exchange_rows(): lax.all_to_all(x, 'expert', split_axis=0, concat_axis=0, tiled=True, axis...  25.1 us
    all_to_all x2, starting transfers between devices, exchange(): lax.all_to_all(x, 'expert', split_axis=0, concat_axis=0, tiled=True, axis...  18.7 us
    ppermute x3, starting transfers between devices, same_side(): pieces.append(lax.ppermute(x, 'expert', pairs))  18 us
    dot_general x4, matrix products, per_device(): projected = jnp.dot(rows_in, gate_up, preferred_element_type=jnp.float32)  10.5 us
    all_to_all x1, starting transfers between devices, exchange_rows(): lax.all_to_all(x, 'expert', split_axis=0, concat_axis=0, tiled=True, axis...  6.87 us
  transfers between devices with their start and end apart: 9, of which 7 were waited for; matrix products, arithmetic and copies ran while one was open for 5% of the time, Pallas kernels for 0%

profile of v2, /device:TPU:56, one launch (start us, length us, event | category | flops | bytes accessed | tf_op | source)
XLA Modules:
  0.0 288.2 jit_solution(9359583662026121123)
XLA Ops:
  0.0 4.3 %collective-permute-start.3 = (bf16[2048,768]{1,0:T(8,128)(2,1)}, bf16[2048,768]{1,0:T(8,128)(2,1)}, u32[]{:S(2)}, u32[]{:S(2)}) collective-permute-start(bf16[2048,768]{1,0:T(8,128)(2,1)} %bitcast.197), channel_id=1, source_target_pairs={{0,1},{1,0},{2,3},{3,2},{4,5},{5,4},{6,7},{7,6},{8,9},{9,8},{10,11... | collective-permute-start | bytes 9437192 | tf_op jit(solution)/shard_map/ppermute | solution.py:70
  4.3 0.7 multiply_bitcast_fusion.1
  6.0 1.0 fusion.29
  7.1 1.0 fusion.31
  8.1 6.1 %collective-permute-start = (bf16[32,2176]{1,0:T(8,128)(2,1)S(1)}, bf16[32,2176]{1,0:T(8,128)(2,1)S(1)}, u32[]{:S(2)}, u32[]{:S(2)}) collective-permute-start(bf16[32,2176]{1,0:T(8,128)(2,1)S(1)} %get-tuple-element.12), channel_id=1, source_target_pairs={{0,2},{1,3},{2,4},{3,5},{4,6},{5,7},{6,0},{7,1},{8,10},{9,11},{10,... | collective-permute-start | bytes 417800 | tf_op jit(solution)/shard_map/ppermute | solution.py:58
  14.2 8.2 %collective-permute-start.1 = (bf16[32,2176]{1,0:T(8,128)(2,1)S(1)}, bf16[32,2176]{1,0:T(8,128)(2,1)S(1)}, u32[]{:S(2)}, u32[]{:S(2)}) collective-permute-start(bf16[32,2176]{1,0:T(8,128)(2,1)S(1)} %get-tuple-element.12), channel_id=1, source_target_pairs={{0,4},{1,5},{2,6},{3,7},{4,0},{5,1},{6,2},{7,3},{8,12},{9,13},{10,... | collective-permute-start | bytes 417800 | tf_op jit(solution)/shard_map/ppermute | solution.py:58
  22.5 3.7 %collective-permute-start.2 = (bf16[32,2176]{1,0:T(8,128)(2,1)S(1)}, bf16[32,2176]{1,0:T(8,128)(2,1)S(1)}, u32[]{:S(2)}, u32[]{:S(2)}) collective-permute-start(bf16[32,2176]{1,0:T(8,128)(2,1)S(1)} %get-tuple-element.12), channel_id=1, source_target_pairs={{0,6},{1,7},{2,0},{3,1},{4,2},{5,3},{6,4},{7,5},{8,14},{9,15},{10,... | collective-permute-start | bytes 417800 | tf_op jit(solution)/shard_map/ppermute | solution.py:58
  26.6 63.0 %collective-permute-done = bf16[32,2176]{1,0:T(8,128)(2,1)S(1)} collective-permute-done((bf16[32,2176]{1,0:T(8,128)(2,1)S(1)}, bf16[32,2176]{1,0:T(8,128)(2,1)S(1)}, u32[]{:S(2)}, u32[]{:S(2)}) %collective-permute-start) | collective-permute-done | bytes 139296 | tf_op jit(solution)/shard_map/ppermute | solution.py:58
  89.6 2.7 collective-permute-done.1
  93.3 1.6 convolution_convert_fusion
  94.9 6.9 %all-to-all-start = ((bf16[8,40,2048]{2,1,0:T(8,128)(2,1)}), bf16[8,40,2048]{2,1,0:T(8,128)(2,1)S(1)}, u32[]{:S(2)}, u32[]{:S(2)}) async-start(bf16[8,40,2048]{2,1,0:T(8,128)(2,1)} %bitcast.13), calls=%async_computation | async-start | bytes 2621440 | tf_op jit(solution)/shard_map/all_to_all | solution.py:65
  101.7 1.9 collective-permute-start.4
  103.7 25.1 %all-to-all-done = bf16[8,40,2048]{2,1,0:T(8,128)(2,1)S(1)} async-done(((bf16[8,40,2048]{2,1,0:T(8,128)(2,1)}), bf16[8,40,2048]{2,1,0:T(8,128)(2,1)S(1)}, u32[]{:S(2)}, u32[]{:S(2)}) %all-to-all-start) | async-done | bytes 1310752 | tf_op jit(solution)/shard_map/all_to_all | solution.py:65
  128.9 3.2 %fusion.14 = f32[320,768]{1,0:T(8,128)S(1)} fusion(bf16[64,2048]{1,0:T(8,128)(2,1)S(1)} %slice_bitcast_fusion.5, bf16[256,2048]{1,0:T(8,128)(2,1)S(1)} %bitcast.172, bf16[1,1,2048,768]{3,2,1,0:T(8,128)(2,1)} %param.10), kind=kOutput, calls=%fused_computation.31 | convolution fusion | flops 1009254400 | bytes 5439488 | tf_op jit(solution)/shard_map/dot_general | solution.py:169
  132.1 0.9 fusion.32
  133.0 3.1 %fusion.13 = f32[320,768]{1,0:T(8,128)S(1)} fusion(bf16[2048,768]{1,0:T(8,128)(2,1)} %collective-permute-done.3, bf16[64,2048]{1,0:T(8,128)(2,1)S(1)} %slice_bitcast_fusion.5, bf16[256,2048]{1,0:T(8,128)(2,1)S(1)} %bitcast.173), kind=kOutput, calls=%fused_computation.30 | convolution fusion | flops 1009254400 | bytes 5439488 | tf_op jit(solution)/shard_map/dot_general | solution.py:169
  136.4 0.9 fusion
  137.8 1.2 pad_maximum_fusion.1
  139.0 10.6 %all-to-all-start.1 = ((bf16[32,160,128]{2,1,0:T(8,128)(2,1)}), bf16[32,160,128]{2,1,0:T(8,128)(2,1)S(1)}, u32[]{:S(2)}, u32[]{:S(2)}) async-start(bf16[32,160,128]{2,1,0:T(8,128)(2,1)} %pad_maximum_fusion.1), calls=%async_computation.1 | async-start | bytes 2621440 | tf_op jit(solution)/shard_map/all_to_all | solution.py:50
  151.0 31.1 %all-to-all-done.1 = bf16[32,160,128]{2,1,0:T(8,128)(2,1)S(1)} async-done(((bf16[32,160,128]{2,1,0:T(8,128)(2,1)}), bf16[32,160,128]{2,1,0:T(8,128)(2,1)S(1)}, u32[]{:S(2)}, u32[]{:S(2)}) %all-to-all-start.1) | async-done | bytes 1310752 | tf_op jit(solution)/shard_map/all_to_all | solution.py:50
  183.5 1.3 collective-permute-start.5
  185.0 0.8 collective-permute-done.5
  187.0 42.9 %all_to_all.20 = bf16[32,160,128]{2,1,0:T(8,128)(2,1)S(1)} all-to-all(bf16[32,160,128]{2,1,0:T(8,128)(2,1)S(1)} %bitcast.165), channel_id=1, replica_groups={{0,2,4,6,8,10,12,14,16,18,20,22,24,26,28,30,32,34,36,38,40,42,44,46,48,..., dimensions={0} | all-to-all | bytes 2621440 | tf_op jit(solution)/shard_map/all_to_all | solution.py:50
  230.8 1.3 copy-done.4
  232.1 1.2 fusion.74
  233.5 0.9 fusion.35
  234.4 3.1 %fusion.82 = f32[320,768]{1,0:T(8,128)S(1)} fusion(bf16[320,2048]{1,0:T(8,128)(2,1)S(1)} %bitcast_dynamic-update-slice_fusion.1, bf16[2048,768]{1,0:T(8,128)(2,1)} %collective-permute-done.3), kind=kOutput, calls=%fused_computation.160 | convolution fusion | flops 1006632960 | bytes 5439488 | tf_op jit(solution)/shard_map/dot_general | solution.py:169
  237.5 0.9 fusion.1
  238.8 1.2 pad_maximum_fusion.2
  240.0 8.1 %all-to-all-start.3 = ((bf16[32,160,128]{2,1,0:T(8,128)(2,1)}), bf16[32,160,128]{2,1,0:T(8,128)(2,1)S(1)}, u32[]{:S(2)}, u32[]{:S(2)}) async-start(bf16[32,160,128]{2,1,0:T(8,128)(2,1)} %pad_maximum_fusion.2), calls=%async_computation.3 | async-start | bytes 2621440 | tf_op jit(solution)/shard_map/all_to_all | solution.py:50
  248.2 38.2 %all-to-all-done.3 = bf16[32,160,128]{2,1,0:T(8,128)(2,1)S(1)} async-done(((bf16[32,160,128]{2,1,0:T(8,128)(2,1)}), bf16[32,160,128]{2,1,0:T(8,128)(2,1)S(1)}, u32[]{:S(2)}, u32[]{:S(2)}) %all-to-all-start.3) | async-done | bytes 1310752 | tf_op jit(solution)/shard_map/all_to_all | solution.py:50
  287.5 0.7 maximum_bitcast_fusion
  (118 shorter events, 9.9 us)
Async XLA Ops:
  0.0 94.9 %collective-permute-start.3 = (bf16[2048,768]{1,0:T(8,128)(2,1)}, bf16[2048,768]{1,0:T(8,128)(2,1)}, u32[]{:S(2)}, u32[]{:S(2)}) collective-permute-start(bf16[2048,768]{1,0:T(8,128)(2,1)} %bitcast.197), channel_id=1, source_target_pairs={{0,1},{1,0},{2,3},{3,2},{4,5},{5,4},{6,7},{7,6},{8,9},{9,8},{10,11... | collective-permute-start | bytes 9437192 | tf_op jit(solution)/shard_map/ppermute | solution.py:70
  8.1 81.5 %collective-permute-start = (bf16[32,2176]{1,0:T(8,128)(2,1)S(1)}, bf16[32,2176]{1,0:T(8,128)(2,1)S(1)}, u32[]{:S(2)}, u32[]{:S(2)}) collective-permute-start(bf16[32,2176]{1,0:T(8,128)(2,1)S(1)} %get-tuple-element.12), channel_id=1, source_target_pairs={{0,2},{1,3},{2,4},{3,5},{4,6},{5,7},{6,0},{7,1},{8,10},{9,11},{10,... | collective-permute-start | bytes 417800 | tf_op jit(solution)/shard_map/ppermute | solution.py:58
  14.2 78.1 %collective-permute-start.1 = (bf16[32,2176]{1,0:T(8,128)(2,1)S(1)}, bf16[32,2176]{1,0:T(8,128)(2,1)S(1)}, u32[]{:S(2)}, u32[]{:S(2)}) collective-permute-start(bf16[32,2176]{1,0:T(8,128)(2,1)S(1)} %get-tuple-element.12), channel_id=1, source_target_pairs={{0,4},{1,5},{2,6},{3,7},{4,0},{5,1},{6,2},{7,3},{8,12},{9,13},{10,... | collective-permute-start | bytes 417800 | tf_op jit(solution)/shard_map/ppermute | solution.py:58
  22.5 69.9 %collective-permute-start.2 = (bf16[32,2176]{1,0:T(8,128)(2,1)S(1)}, bf16[32,2176]{1,0:T(8,128)(2,1)S(1)}, u32[]{:S(2)}, u32[]{:S(2)}) collective-permute-start(bf16[32,2176]{1,0:T(8,128)(2,1)S(1)} %get-tuple-element.12), channel_id=1, source_target_pairs={{0,6},{1,7},{2,0},{3,1},{4,2},{5,3},{6,4},{7,5},{8,14},{9,15},{10,... | collective-permute-start | bytes 417800 | tf_op jit(solution)/shard_map/ppermute | solution.py:58
  94.9 33.9 %all-to-all-start = ((bf16[8,40,2048]{2,1,0:T(8,128)(2,1)}), bf16[8,40,2048]{2,1,0:T(8,128)(2,1)S(1)}, u32[]{:S(2)}, u32[]{:S(2)}) async-start(bf16[8,40,2048]{2,1,0:T(8,128)(2,1)} %bitcast.13), calls=%async_computation | async-start | bytes 2621440 | tf_op jit(solution)/shard_map/all_to_all | solution.py:65
  101.7 34.7 %collective-permute-start.4 = (bf16[384,2048]{1,0:T(8,128)(2,1)}, bf16[384,2048]{1,0:T(8,128)(2,1)S(1)}, u32[]{:S(2)}, u32[]{:S(2)}) collective-permute-start(bf16[384,2048]{1,0:T(8,128)(2,1)} %bitcast.198), channel_id=1, source_target_pairs={{0,1},{1,0},{2,3},{3,2},{4,5},{5,4},{6,7},{7,6},{8,9},{9,8},{10,11... | collective-permute-start | bytes 4718600 | tf_op jit(solution)/shard_map/ppermute | solution.py:70
  128.9 3.2 %copy-start.5 = (bf16[1,1,384,2048]{3,2,1,0:T(8,128)(2,1)S(1)}, bf16[1,1,384,2048]{3,2,1,0:T(8,128)(2,1)}, u32[]{:S(2)}) copy-start(bf16[1,1,384,2048]{3,2,1,0:T(8,128)(2,1)} %param.11) | copy-start | bytes 4718596
  139.0 11.8 %copy-start.3 = (f32[2,1,32,4]{2,3,1,0:T(4,128)S(1)}, f32[2,1,32,4]{2,3,1,0:T(4,128)}, u32[]{:S(2)}) copy-start(f32[2,1,32,4]{2,3,1,0:T(4,128)} %param.13) | copy-start | bytes 3076
  139.0 43.0 %all-to-all-start.1 = ((bf16[32,160,128]{2,1,0:T(8,128)(2,1)}), bf16[32,160,128]{2,1,0:T(8,128)(2,1)S(1)}, u32[]{:S(2)}, u32[]{:S(2)}) async-start(bf16[32,160,128]{2,1,0:T(8,128)(2,1)} %pad_maximum_fusion.1), calls=%async_computation.1 | async-start | bytes 2621440 | tf_op jit(solution)/shard_map/all_to_all | solution.py:50
  182.4 0.9 copy-start
  182.8 3.0 %copy-start.1 = (bf16[1,32,2048]{2,1,0:T(8,128)(2,1)S(1)}, bf16[1,32,2048]{2,1,0:T(8,128)(2,1)}, u32[]{:S(2)}) copy-start(bf16[1,32,2048]{2,1,0:T(8,128)(2,1)} %param.8) | copy-start | bytes 393220
  182.8 3.2 %copy-start.2 = (f32[1,2048]{1,0:T(1,128)S(1)}, f32[1,2048]{1,0:T(1,128)}, u32[]{:S(2)}) copy-start(f32[1,2048]{1,0:T(1,128)} %param.9) | copy-start | bytes 24580
  183.5 2.3 collective-permute-start.5
  230.2 1.9 copy-start.4
  232.1 1.4 copy-start.6
  240.0 46.4 %all-to-all-start.3 = ((bf16[32,160,128]{2,1,0:T(8,128)(2,1)}), bf16[32,160,128]{2,1,0:T(8,128)(2,1)S(1)}, u32[]{:S(2)}, u32[]{:S(2)}) async-start(bf16[32,160,128]{2,1,0:T(8,128)(2,1)} %pad_maximum_fusion.2), calls=%async_computation.3 | async-start | bytes 2621440 | tf_op jit(solution)/shard_map/all_to_all | solution.py:50

commit v3 on v2

--- a/solution.py
+++ b/solution.py
@@ -68,6 +68,12 @@
 def swapped(x):
     length = lax.axis_size("expert")
     return lax.ppermute(x, "expert", [(i, i ^ 1) for i in range(length)])
+
+
+def gated(rows, weights):
+    half = weights.shape[1] // 2
+    projected = jnp.dot(rows, weights, preferred_element_type=jnp.float32)
+    return (jax.nn.silu(projected[:, :half]) * projected[:, half:]).astype(jnp.bfloat16)
 
 
 def first_dispatch(normed, chosen, parts, column, expert_count, swapped_first):
@@ -80,6 +86,7 @@
     slot_at = jnp.sum(jnp.where(named, slot[:, :, None] + 1, 0), axis=1)
     slot_at = jnp.pad(slot_at, ((0, 0), (0, LANES - expert_count))).astype(jnp.bfloat16)
     everyone = same_side(jnp.concatenate([normed, slot_at], axis=1))
+    everyone, _ = lax.optimization_barrier((everyone, swapped_first))
     mine = column // SHARE
     position = (mine - jnp.arange(sources, dtype=jnp.int32)) % sources
     origin = jnp.arange(sources, dtype=jnp.int32)[:, None] == position[None, :]
@@ -98,7 +105,6 @@
     flat = everyone[:, :, :width].reshape(sources * tokens, width)
     packed = jnp.dot(picker.reshape(rows_of_chips * count, sources * tokens), flat, preferred_element_type=jnp.float32)
     packed = packed.astype(jnp.bfloat16).reshape(rows_of_chips, count, width)
-    packed, _ = lax.optimization_barrier((packed, swapped_first))
     received = exchange_rows(packed)
     rows_in = []
     first = 0
@@ -121,11 +127,13 @@
         high = min(low + ROWS, capacity)
         parts.append((low, high))
         low = high
-    hidden_width = w_down.shape[2]
     column = lax.axis_index("expert") % COLUMNS
     section_index = lax.axis_index("section")
-    gate_up_weights = [w_gate_up[0, 0], swapped(w_gate_up[0, 0])]
-    down_weights = [w_down[0, 0], swapped(w_down[0, 0])]
+    gate_up_own, down_own = w_gate_up[0, 0], w_down[0, 0]
+    wide = gate_up_own.shape[1]
+    down_last = swapped(down_own[:, wide:])
+    joined = swapped(jnp.concatenate([gate_up_own, down_own[:, :wide]], axis=0))
+    gate_up_other, down_first = joined[:gate_up_own.shape[0]], joined[gate_up_own.shape[0]:]
     gain_values = norm_gain[0]
     plans = []
     for tick_index in range(TICKS):
@@ -155,7 +163,7 @@
         for low, high in parts:
             at.append(at[-1] + (high - low) * normed.shape[1] // LANES)
         if tick_index == 0:
-            rows_in = first_dispatch(normed, routes[0, 0], parts, column, expert_count, gate_up_weights[1])
+            rows_in = first_dispatch(normed, routes[0, 0], parts, column, expert_count, down_last)
         else:
             sent = []
             for (low, high), (picker, _, _) in zip(parts, plan):
@@ -164,11 +172,11 @@
             received = exchange(jnp.repeat(jnp.concatenate(sent, axis=1), copies, axis=0))
             rows_in = [from_tiles(received[:, at[i]:at[i + 1]], high - low) for i, (low, high) in enumerate(parts)]
             rows_in = jnp.concatenate(rows_in, axis=0)
-        partial_value = 0.0
-        for gate_up, down in zip(gate_up_weights, down_weights):
-            projected = jnp.dot(rows_in, gate_up, preferred_element_type=jnp.float32)
-            hidden = (jax.nn.silu(projected[:, :hidden_width]) * projected[:, hidden_width:]).astype(jnp.bfloat16)
-            partial_value = partial_value + jnp.dot(hidden, down, preferred_element_type=jnp.float32)
+        hidden_own = gated(rows_in, gate_up_own)
+        hidden_other = gated(rows_in, gate_up_other)
+        down_other = jnp.concatenate([down_first, down_last], axis=1)
+        partial_value = jnp.dot(hidden_own, down_own, preferred_element_type=jnp.float32)
+        partial_value = partial_value + jnp.dot(hidden_other, down_other, preferred_element_type=jnp.float32)
         partial_value = partial_value.astype(jnp.bfloat16)
         split = [partial_value[group * low:group * high] for low, high in parts]
         back = exchange(jnp.concatenate([to_tiles(piece, group) for piece in split], axis=1))

time: 289 us -> 292 us (1.010)
  blocking collectives: 42.9 us -> 80.1 us
  waiting for transfers between devices: 161 us -> 128 us
  starting transfers between devices: 51 us -> 42 us
  local copies, waits for them, and re-layouts: 6.3 us -> 10.8 us
    ppermute x3, waiting for transfers between devices: 65.8 us -> 0.01 us  [same_side(): pieces.append(lax.ppermute(x, 'expert', pairs))]
    ppermute x2, waiting for transfers between devices: 0.39 us -> 58.7 us  [swapped(): return lax.ppermute(x, 'expert', [(i, i ^ 1) for i in range(length)])]
    all_to_all x0 -> x1, blocking collectives: none -> 36.4 us  [exchange_rows(): lax.all_to_all(x, 'expert', split_axis=0, concat_axis=0, tiled=True, axis...]
    all_to_all x1 -> x0, waiting for transfers between devices: 25.1 us -> none  [exchange_rows(): lax.all_to_all(x, 'expert', split_axis=0, concat_axis=0, tiled=True, axis...]
    all_to_all x1 -> x0, starting transfers between devices: 6.87 us -> none  [exchange_rows(): lax.all_to_all(x, 'expert', split_axis=0, concat_axis=0, tiled=True, axis...]
    slice x0 -> x4, local copies, waits for them, and re-layouts: none -> 3.67 us  [the longest x1 1.42 us: per_device(): down_last = swapped(down_own[:, wide:])]
  transfers between devices with their start and end apart: 9 -> 8, of which waited for: 7 -> 5; matrix products, arithmetic and copies ran while one was open for 5% -> 4% of each run, Pallas kernels for 0% -> 0%
where the time goes in v3:
time: 292 us; the launch traced here: 290 us
  waiting for transfers between devices  128 us (44%)
  blocking collectives  80.1 us (27%)
  starting transfers between devices  42 us (14%)
  matrix products  17.5 us (6%)
  local copies, waits for them, and re-layouts  10.8 us (4%)
  other arithmetic  10.2 us (3%)
    all_to_all x2, waiting for transfers between devices, exchange(): lax.all_to_all(x, 'expert', split_axis=0, concat_axis=0, tiled=True, axis...  69 us
    ppermute x2, waiting for transfers between devices, swapped(): return lax.ppermute(x, 'expert', [(i, i ^ 1) for i in range(length)])  58.7 us
    all_to_all x1, blocking collectives, exchange(): lax.all_to_all(x, 'expert', split_axis=0, concat_axis=0, tiled=True, axis...  43.7 us
    all_to_all x1, blocking collectives, exchange_rows(): lax.all_to_all(x, 'expert', split_axis=0, concat_axis=0, tiled=True, axis...  36.4 us
    ppermute x3, starting transfers between devices, same_side(): pieces.append(lax.ppermute(x, 'expert', pairs))  18.9 us
    all_to_all x2, starting transfers between devices, exchange(): lax.all_to_all(x, 'expert', split_axis=0, concat_axis=0, tiled=True, axis...  16 us
    dot_general x4, matrix products, gated(): projected = jnp.dot(rows, weights, preferred_element_type=jnp.float32)  8.56 us
  transfers between devices with their start and end apart: 8, of which 5 were waited for; matrix products, arithmetic and copies ran while one was open for 4% of the time, Pallas kernels for 0%

profile of v3, /device:TPU:56, one launch (start us, length us, event | category | flops | bytes accessed | tf_op | source)
XLA Modules:
  0.0 289.7 jit_solution(368803627249949175)
XLA Ops:
  1.8 1.0 fusion.32
  2.8 1.0 fusion.34
  3.9 6.1 %collective-permute-start = (bf16[32,2176]{1,0:T(8,128)(2,1)S(1)}, bf16[32,2176]{1,0:T(8,128)(2,1)S(1)}, u32[]{:S(2)}, u32[]{:S(2)}) collective-permute-start(bf16[32,2176]{1,0:T(8,128)(2,1)S(1)} %get-tuple-element.12), channel_id=1, source_target_pairs={{0,2},{1,3},{2,4},{3,5},{4,6},{5,7},{6,0},{7,1},{8,10},{9,11},{10,... | collective-permute-start | bytes 417800 | tf_op jit(solution)/shard_map/ppermute | solution.py:58
  10.0 9.1 %collective-permute-start.1 = (bf16[32,2176]{1,0:T(8,128)(2,1)S(1)}, bf16[32,2176]{1,0:T(8,128)(2,1)S(1)}, u32[]{:S(2)}, u32[]{:S(2)}) collective-permute-start(bf16[32,2176]{1,0:T(8,128)(2,1)S(1)} %get-tuple-element.12), channel_id=1, source_target_pairs={{0,4},{1,5},{2,6},{3,7},{4,0},{5,1},{6,2},{7,3},{8,12},{9,13},{10,... | collective-permute-start | bytes 417800 | tf_op jit(solution)/shard_map/ppermute | solution.py:58
  19.1 3.7 %collective-permute-start.2 = (bf16[32,2176]{1,0:T(8,128)(2,1)S(1)}, bf16[32,2176]{1,0:T(8,128)(2,1)S(1)}, u32[]{:S(2)}, u32[]{:S(2)}) collective-permute-start(bf16[32,2176]{1,0:T(8,128)(2,1)S(1)} %get-tuple-element.12), channel_id=1, source_target_pairs={{0,6},{1,7},{2,0},{3,1},{4,2},{5,3},{6,4},{7,5},{8,14},{9,15},{10,... | collective-permute-start | bytes 417800 | tf_op jit(solution)/shard_map/ppermute | solution.py:58
  22.8 1.4 slice.121
  24.2 3.4 %collective-permute-start.3 = (bf16[384,1280]{1,0:T(8,128)(2,1)S(1)}, bf16[384,1280]{1,0:T(8,128)(2,1)}, u32[]{:S(2)}, u32[]{:S(2)}) collective-permute-start(bf16[384,1280]{1,0:T(8,128)(2,1)S(1)} %slice.121), channel_id=1, source_target_pairs={{0,1},{1,0},{2,3},{3,2},{4,5},{5,4},{6,7},{7,6},{8,9},{9,8},{10,11... | collective-permute-start | bytes 2949128 | tf_op jit(solution)/shard_map/ppermute | solution.py:70
  27.6 1.1 slice.127
  28.7 2.1 pad_maximum_fusion
  30.8 2.5 collective-permute-start.4
  33.8 20.0 %collective-permute-done.3 = bf16[384,1280]{1,0:T(8,128)(2,1)} collective-permute-done((bf16[384,1280]{1,0:T(8,128)(2,1)S(1)}, bf16[384,1280]{1,0:T(8,128)(2,1)}, u32[]{:S(2)}, u32[]{:S(2)}) %collective-permute-start.3) | collective-permute-done | bytes 983072 | tf_op jit(solution)/shard_map/ppermute | solution.py:70
  53.8 1.1 copy.231
  56.3 36.4 %all_to_all.20 = bf16[8,40,2048]{2,1,0:T(8,128)(2,1)S(1)} all-to-all(bf16[8,40,2048]{2,1,0:T(8,128)(2,1)S(1)} %bitcast.161), channel_id=1, replica_groups={{0,8,16,24,32,40,48,56},{1,9,17,25,33,41,49,57},{2,10,18,26,34,42,50,58..., dimensions={0} | all-to-all | bytes 2621440 | tf_op jit(solution)/shard_map/all_to_all | solution.py:65
  92.9 1.2 fusion.17
  94.3 0.9 fusion.35
  95.1 38.7 %collective-permute-done.4 = bf16[2432,768]{1,0:T(8,128)(2,1)} collective-permute-done((bf16[2432,768]{1,0:T(8,128)(2,1)}, bf16[2432,768]{1,0:T(8,128)(2,1)}, u32[]{:S(2)}, u32[]{:S(2)}) %collective-permute-start.4) | collective-permute-done | bytes 3735584 | tf_op jit(solution)/shard_map/ppermute | solution.py:70
  133.8 3.1 %fusion.2 = f32[320,768]{1,0:T(8,128)S(1)} fusion(bf16[2432,768]{1,0:T(8,128)(2,1)} %collective-permute-done.4, bf16[64,2048]{1,0:T(8,128)(2,1)S(1)} %slice_bitcast_fusion.5, bf16[256,2048]{1,0:T(8,128)(2,1)S(1)} %bitcast.173), kind=kOutput, calls=%fused_computation.5 | convolution fusion | flops 1009254400 | bytes 5439488 | tf_op jit(solution)/shard_map/dot_general | solution.py:75
  136.9 1.1 slice.131
  138.0 2.3 fusion.4
  140.7 1.2 pad_maximum_fusion.3
  141.9 8.5 %all-to-all-start.1 = ((bf16[32,160,128]{2,1,0:T(8,128)(2,1)}), bf16[32,160,128]{2,1,0:T(8,128)(2,1)S(1)}, u32[]{:S(2)}, u32[]{:S(2)}) async-start(bf16[32,160,128]{2,1,0:T(8,128)(2,1)} %pad_maximum_fusion.3), calls=%async_computation.1 | async-start | bytes 2621440 | tf_op jit(solution)/shard_map/all_to_all | solution.py:50
  151.7 31.0 %all-to-all-done.1 = bf16[32,160,128]{2,1,0:T(8,128)(2,1)S(1)} async-done(((bf16[32,160,128]{2,1,0:T(8,128)(2,1)}), bf16[32,160,128]{2,1,0:T(8,128)(2,1)S(1)}, u32[]{:S(2)}, u32[]{:S(2)}) %all-to-all-start.1) | async-done | bytes 1310752 | tf_op jit(solution)/shard_map/all_to_all | solution.py:50
  184.0 1.3 collective-permute-start.5
  187.4 43.7 %all_to_all.21 = bf16[32,160,128]{2,1,0:T(8,128)(2,1)S(1)} all-to-all(bf16[32,160,128]{2,1,0:T(8,128)(2,1)S(1)} %bitcast.162), channel_id=1, replica_groups={{0,2,4,6,8,10,12,14,16,18,20,22,24,26,28,30,32,34,36,38,40,42,44,46,48,..., dimensions={0} | all-to-all | bytes 2621440 | tf_op jit(solution)/shard_map/all_to_all | solution.py:50
  232.1 1.3 copy-done.2
  233.4 1.2 fusion.77
  234.6 0.9 fusion.38
  235.4 3.1 %fusion = f32[320,768]{1,0:T(8,128)S(1)} fusion(bf16[320,2048]{1,0:T(8,128)(2,1)S(1)} %bitcast_dynamic-update-slice_fusion.1, bf16[2432,768]{1,0:T(8,128)(2,1)} %collective-permute-done.4), kind=kOutput, calls=%fused_computation.3 | convolution fusion | flops 1006632960 | bytes 5439488 | tf_op jit(solution)/shard_map/dot_general | solution.py:75
  238.6 2.1 fusion.5
  241.1 1.2 pad_maximum_fusion.4
  242.2 7.5 %all-to-all-start.3 = ((bf16[32,160,128]{2,1,0:T(8,128)(2,1)}), bf16[32,160,128]{2,1,0:T(8,128)(2,1)S(1)}, u32[]{:S(2)}, u32[]{:S(2)}) async-start(bf16[32,160,128]{2,1,0:T(8,128)(2,1)} %pad_maximum_fusion.4), calls=%async_computation.3 | async-start | bytes 2621440 | tf_op jit(solution)/shard_map/all_to_all | solution.py:50
  249.8 38.0 %all-to-all-done.3 = bf16[32,160,128]{2,1,0:T(8,128)(2,1)S(1)} async-done(((bf16[32,160,128]{2,1,0:T(8,128)(2,1)}), bf16[32,160,128]{2,1,0:T(8,128)(2,1)S(1)}, u32[]{:S(2)}, u32[]{:S(2)}) %all-to-all-start.3) | async-done | bytes 1310752 | tf_op jit(solution)/shard_map/all_to_all | solution.py:50
  (127 shorter events, 12.0 us)
Async XLA Ops:
  3.9 29.8 %collective-permute-start = (bf16[32,2176]{1,0:T(8,128)(2,1)S(1)}, bf16[32,2176]{1,0:T(8,128)(2,1)S(1)}, u32[]{:S(2)}, u32[]{:S(2)}) collective-permute-start(bf16[32,2176]{1,0:T(8,128)(2,1)S(1)} %get-tuple-element.12), channel_id=1, source_target_pairs={{0,2},{1,3},{2,4},{3,5},{4,6},{5,7},{6,0},{7,1},{8,10},{9,11},{10,... | collective-permute-start | bytes 417800 | tf_op jit(solution)/shard_map/ppermute | solution.py:58
  10.0 23.7 %collective-permute-start.1 = (bf16[32,2176]{1,0:T(8,128)(2,1)S(1)}, bf16[32,2176]{1,0:T(8,128)(2,1)S(1)}, u32[]{:S(2)}, u32[]{:S(2)}) collective-permute-start(bf16[32,2176]{1,0:T(8,128)(2,1)S(1)} %get-tuple-element.12), channel_id=1, source_target_pairs={{0,4},{1,5},{2,6},{3,7},{4,0},{5,1},{6,2},{7,3},{8,12},{9,13},{10,... | collective-permute-start | bytes 417800 | tf_op jit(solution)/shard_map/ppermute | solution.py:58
  19.1 14.6 %collective-permute-start.2 = (bf16[32,2176]{1,0:T(8,128)(2,1)S(1)}, bf16[32,2176]{1,0:T(8,128)(2,1)S(1)}, u32[]{:S(2)}, u32[]{:S(2)}) collective-permute-start(bf16[32,2176]{1,0:T(8,128)(2,1)S(1)} %get-tuple-element.12), channel_id=1, source_target_pairs={{0,6},{1,7},{2,0},{3,1},{4,2},{5,3},{6,4},{7,5},{8,14},{9,15},{10,... | collective-permute-start | bytes 417800 | tf_op jit(solution)/shard_map/ppermute | solution.py:58
  22.7 5.9 %copy-start = (bf16[1,1,2048,768]{3,2,1,0:T(8,128)(2,1)S(1)}, bf16[1,1,2048,768]{3,2,1,0:T(8,128)(2,1)}, u32[]{:S(2)}) copy-start(bf16[1,1,2048,768]{3,2,1,0:T(8,128)(2,1)} %param.10) | copy-start | bytes 9437188
  24.2 29.6 %collective-permute-start.3 = (bf16[384,1280]{1,0:T(8,128)(2,1)S(1)}, bf16[384,1280]{1,0:T(8,128)(2,1)}, u32[]{:S(2)}, u32[]{:S(2)}) collective-permute-start(bf16[384,1280]{1,0:T(8,128)(2,1)S(1)} %slice.121), channel_id=1, source_target_pairs={{0,1},{1,0},{2,3},{3,2},{4,5},{5,4},{6,7},{7,6},{8,9},{9,8},{10,11... | collective-permute-start | bytes 2949128 | tf_op jit(solution)/shard_map/ppermute | solution.py:70
  30.8 103.0 %collective-permute-start.4 = (bf16[2432,768]{1,0:T(8,128)(2,1)}, bf16[2432,768]{1,0:T(8,128)(2,1)}, u32[]{:S(2)}, u32[]{:S(2)}) collective-permute-start(bf16[2432,768]{1,0:T(8,128)(2,1)} %pad_maximum_fusion), channel_id=1, source_target_pairs={{0,1},{1,0},{2,3},{3,2},{4,5},{5,4},{6,7},{7,6},{8,9},{9,8},{10,11... | collective-permute-start | bytes 11206664 | tf_op jit(solution)/shard_map/ppermute | solution.py:70
  56.3 36.5 %copy-start.1 = (bf16[1,1,2048,768]{3,2,1,0:T(8,128)(2,1)S(1)}, bf16[1,1,2048,768]{3,2,1,0:T(8,128)(2,1)}, u32[]{:S(2)}) copy-start(bf16[1,1,2048,768]{3,2,1,0:T(8,128)(2,1)} %param.10) | copy-start | bytes 9437188
  92.8 1.4 copy-start.3
  138.0 2.5 copy-start.5
  141.9 9.7 %copy-start.9 = (f32[2,1,32,4]{2,3,1,0:T(4,128)S(1)}, f32[2,1,32,4]{2,3,1,0:T(4,128)}, u32[]{:S(2)}) copy-start(f32[2,1,32,4]{2,3,1,0:T(4,128)} %param.13) | copy-start | bytes 3076
  141.9 40.8 %all-to-all-start.1 = ((bf16[32,160,128]{2,1,0:T(8,128)(2,1)}), bf16[32,160,128]{2,1,0:T(8,128)(2,1)S(1)}, u32[]{:S(2)}, u32[]{:S(2)}) async-start(bf16[32,160,128]{2,1,0:T(8,128)(2,1)} %pad_maximum_fusion.3), calls=%async_computation.1 | async-start | bytes 2621440 | tf_op jit(solution)/shard_map/all_to_all | solution.py:50
  182.9 0.9 copy-start.4
  183.4 2.8 copy-start.7
  183.5 3.0 %copy-start.8 = (f32[1,2048]{1,0:T(1,128)S(1)}, f32[1,2048]{1,0:T(1,128)}, u32[]{:S(2)}) copy-start(f32[1,2048]{1,0:T(1,128)} %param.9) | copy-start | bytes 24580
  184.0 2.3 collective-permute-start.5
  231.5 1.9 copy-start.2
  235.4 3.1 %copy-start.6 = (bf16[384,768]{1,0:T(8,128)(2,1)S(1)}, bf16[384,768]{1,0:T(8,128)(2,1)}, u32[]{:S(2)}) copy-start(bf16[384,768]{1,0:T(8,128)(2,1)} %copy-done.5) | copy-start | bytes 1769476
  242.2 45.6 %all-to-all-start.3 = ((bf16[32,160,128]{2,1,0:T(8,128)(2,1)}), bf16[32,160,128]{2,1,0:T(8,128)(2,1)S(1)}, u32[]{:S(2)}, u32[]{:S(2)}) async-start(bf16[32,160,128]{2,1,0:T(8,128)(2,1)} %pad_maximum_fusion.4), calls=%async_computation.3 | async-start | bytes 2621440 | tf_op jit(solution)/shard_map/all_to_all | solution.py:50

commit v4 on v3

--- a/solution.py
+++ b/solution.py
@@ -130,10 +130,8 @@
     column = lax.axis_index("expert") % COLUMNS
     section_index = lax.axis_index("section")
     gate_up_own, down_own = w_gate_up[0, 0], w_down[0, 0]
-    wide = gate_up_own.shape[1]
-    down_last = swapped(down_own[:, wide:])
-    joined = swapped(jnp.concatenate([gate_up_own, down_own[:, :wide]], axis=0))
-    gate_up_other, down_first = joined[:gate_up_own.shape[0]], joined[gate_up_own.shape[0]:]
+    down_other = swapped(down_own)
+    gate_up_other = swapped(gate_up_own)
     gain_values = norm_gain[0]
     plans = []
     for tick_index in range(TICKS):
@@ -163,7 +161,8 @@
         for low, high in parts:
             at.append(at[-1] + (high - low) * normed.shape[1] // LANES)
         if tick_index == 0:
-            rows_in = first_dispatch(normed, routes[0, 0], parts, column, expert_count, down_last)
+            rows_in = first_dispatch(normed, routes[0, 0], parts, column, expert_count, down_other)
+            rows_in, gate_up_other = lax.optimization_barrier((rows_in, gate_up_other))
         else:
             sent = []
             for (low, high), (picker, _, _) in zip(parts, plan):
@@ -174,7 +173,6 @@
             rows_in = jnp.concatenate(rows_in, axis=0)
         hidden_own = gated(rows_in, gate_up_own)
         hidden_other = gated(rows_in, gate_up_other)
-        down_other = jnp.concatenate([down_first, down_last], axis=1)
         partial_value = jnp.dot(hidden_own, down_own, preferred_element_type=jnp.float32)
         partial_value = partial_value + jnp.dot(hidden_other, down_other, preferred_element_type=jnp.float32)
         partial_value = partial_value.astype(jnp.bfloat16)

time: 292 us -> 279 us (0.955)
  starting transfers between devices: 42 us -> 49.3 us
  waiting for transfers between devices: 128 us -> 121 us
  blocking collectives: 80.1 us -> 75.2 us
  local copies, waits for them, and re-layouts: 10.8 us -> 6.83 us
    ppermute x2, waiting for transfers between devices: 58.7 us -> 22.2 us  [swapped(): return lax.ppermute(x, 'expert', [(i, i ^ 1) for i in range(length)])]
    ppermute x3, waiting for transfers between devices: 0.01 us -> 30.7 us  [same_side(): pieces.append(lax.ppermute(x, 'expert', pairs))]
    all_to_all x2, starting transfers between devices: 16 us -> 23.3 us  [exchange(): lax.all_to_all(x, 'expert', split_axis=0, concat_axis=0, tiled=True, axis...]
    all_to_all x1, blocking collectives: 36.4 us -> 32.1 us  [exchange_rows(): lax.all_to_all(x, 'expert', split_axis=0, concat_axis=0, tiled=True, axis...]
    slice x3 -> x0, local copies, waits for them, and re-layouts: 3.63 us -> none  [the longest x1 1.42 us: per_device(): down_last = swapped(down_own[:, wide:])]
  transfers between devices with their start and end apart: 8 -> 8, of which waited for: 5 -> 6; matrix products, arithmetic and copies ran while one was open for 4% -> 4% of each run, Pallas kernels for 0% -> 0%
where the time goes in v4:
time: 279 us; the launch traced here: 278 us
  waiting for transfers between devices  121 us (43%)
  blocking collectives  75.2 us (27%)
  starting transfers between devices  49.3 us (18%)
  matrix products  15.2 us (5%)
  other arithmetic  8.94 us (3%)
  local copies, waits for them, and re-layouts  6.83 us (2%)
    all_to_all x2, waiting for transfers between devices, exchange(): lax.all_to_all(x, 'expert', split_axis=0, concat_axis=0, tiled=True, axis...  67.6 us
    all_to_all x1, blocking collectives, exchange(): lax.all_to_all(x, 'expert', split_axis=0, concat_axis=0, tiled=True, axis...  43.1 us
    all_to_all x1, blocking collectives, exchange_rows(): lax.all_to_all(x, 'expert', split_axis=0, concat_axis=0, tiled=True, axis...  32.1 us
    ppermute x3, waiting for transfers between devices, same_side(): pieces.append(lax.ppermute(x, 'expert', pairs))  30.7 us
    all_to_all x2, starting transfers between devices, exchange(): lax.all_to_all(x, 'expert', split_axis=0, concat_axis=0, tiled=True, axis...  23.3 us
    ppermute x2, waiting for transfers between devices, swapped(): return lax.ppermute(x, 'expert', [(i, i ^ 1) for i in range(length)])  22.2 us
    ppermute x3, starting transfers between devices, same_side(): pieces.append(lax.ppermute(x, 'expert', pairs))  18 us
    dot_general x4, matrix products, gated(): projected = jnp.dot(rows, weights, preferred_element_type=jnp.float32)  8.85 us
  transfers between devices with their start and end apart: 8, of which 6 were waited for; matrix products, arithmetic and copies ran while one was open for 4% of the time, Pallas kernels for 0%

profile of v4, /device:TPU:56, one launch (start us, length us, event | category | flops | bytes accessed | tf_op | source)
XLA Modules:
  0.0 277.6 jit_solution(13639979172553232408)
XLA Ops:
  0.0 4.3 %collective-permute-start.3 = (bf16[384,2048]{1,0:T(8,128)(2,1)}, bf16[384,2048]{1,0:T(8,128)(2,1)S(1)}, u32[]{:S(2)}, u32[]{:S(2)}) collective-permute-start(bf16[384,2048]{1,0:T(8,128)(2,1)} %bitcast.197), channel_id=1, source_target_pairs={{0,1},{1,0},{2,3},{3,2},{4,5},{5,4},{6,7},{7,6},{8,9},{9,8},{10,11... | collective-permute-start | bytes 4718600 | tf_op jit(solution)/shard_map/ppermute | solution.py:70
  4.3 0.7 multiply_bitcast_fusion.1
  6.0 1.0 fusion.27
  7.1 1.0 fusion.29
  8.1 6.1 %collective-permute-start = (bf16[32,2176]{1,0:T(8,128)(2,1)S(1)}, bf16[32,2176]{1,0:T(8,128)(2,1)S(1)}, u32[]{:S(2)}, u32[]{:S(2)}) collective-permute-start(bf16[32,2176]{1,0:T(8,128)(2,1)S(1)} %get-tuple-element.16), channel_id=1, source_target_pairs={{0,2},{1,3},{2,4},{3,5},{4,6},{5,7},{6,0},{7,1},{8,10},{9,11},{10,... | collective-permute-start | bytes 417800 | tf_op jit(solution)/shard_map/ppermute | solution.py:58
  14.2 8.2 %collective-permute-start.1 = (bf16[32,2176]{1,0:T(8,128)(2,1)S(1)}, bf16[32,2176]{1,0:T(8,128)(2,1)S(1)}, u32[]{:S(2)}, u32[]{:S(2)}) collective-permute-start(bf16[32,2176]{1,0:T(8,128)(2,1)S(1)} %get-tuple-element.16), channel_id=1, source_target_pairs={{0,4},{1,5},{2,6},{3,7},{4,0},{5,1},{6,2},{7,3},{8,12},{9,13},{10,... | collective-permute-start | bytes 417800 | tf_op jit(solution)/shard_map/ppermute | solution.py:58
  22.5 3.7 %collective-permute-start.2 = (bf16[32,2176]{1,0:T(8,128)(2,1)S(1)}, bf16[32,2176]{1,0:T(8,128)(2,1)S(1)}, u32[]{:S(2)}, u32[]{:S(2)}) collective-permute-start(bf16[32,2176]{1,0:T(8,128)(2,1)S(1)} %get-tuple-element.16), channel_id=1, source_target_pairs={{0,6},{1,7},{2,0},{3,1},{4,2},{5,3},{6,4},{7,5},{8,14},{9,15},{10,... | collective-permute-start | bytes 417800 | tf_op jit(solution)/shard_map/ppermute | solution.py:58
  26.1 2.5 collective-permute-start.4
  29.1 26.7 %collective-permute-done = bf16[32,2176]{1,0:T(8,128)(2,1)S(1)} collective-permute-done((bf16[32,2176]{1,0:T(8,128)(2,1)S(1)}, bf16[32,2176]{1,0:T(8,128)(2,1)S(1)}, u32[]{:S(2)}, u32[]{:S(2)}) %collective-permute-start) | collective-permute-done | bytes 139296 | tf_op jit(solution)/shard_map/ppermute | solution.py:58
  55.7 4.0 %collective-permute-done.1 = bf16[32,2176]{1,0:T(8,128)(2,1)S(1)} collective-permute-done((bf16[32,2176]{1,0:T(8,128)(2,1)S(1)}, bf16[32,2176]{1,0:T(8,128)(2,1)S(1)}, u32[]{:S(2)}, u32[]{:S(2)}) %collective-permute-start.1) | collective-permute-done | bytes 139296 | tf_op jit(solution)/shard_map/ppermute | solution.py:58
  59.9 1.8 copy.231
  61.8 0.7 convert_add_fusion
  63.8 32.1 %all_to_all.20 = bf16[8,40,2048]{2,1,0:T(8,128)(2,1)S(1)} all-to-all(bf16[8,40,2048]{2,1,0:T(8,128)(2,1)S(1)} %bitcast.167), channel_id=1, replica_groups={{0,8,16,24,32,40,48,56},{1,9,17,25,33,41,49,57},{2,10,18,26,34,42,50,58..., dimensions={0} | all-to-all | bytes 2621440 | tf_op jit(solution)/shard_map/all_to_all | solution.py:65
  96.1 22.2 %collective-permute-done.4 = bf16[2048,768]{1,0:T(8,128)(2,1)} collective-permute-done((bf16[2048,768]{1,0:T(8,128)(2,1)}, bf16[2048,768]{1,0:T(8,128)(2,1)}, u32[]{:S(2)}, u32[]{:S(2)}) %collective-permute-start.4) | collective-permute-done | bytes 3145760 | tf_op jit(solution)/shard_map/ppermute | solution.py:70
  118.3 1.2 fusion.70
  119.5 3.2 %fusion.79 = f32[320,768]{1,0:T(8,128)S(1)} fusion(bf16[320,2048]{1,0:T(8,128)(2,1)S(1)} %pad_maximum_fusion, bf16[2048,768]{1,0:T(8,128)(2,1)} %collective-permute-done.4), kind=kOutput, calls=%fused_computation.154 | convolution fusion | flops 1006632960 | bytes 5439488 | tf_op jit(solution)/shard_map/dot_general | solution.py:75
  122.7 0.9 fusion.30
  123.6 0.9 fusion
  125.0 1.2 pad_maximum_fusion.1
  126.1 15.1 %all-to-all-start.1 = ((bf16[32,160,128]{2,1,0:T(8,128)(2,1)}), bf16[32,160,128]{2,1,0:T(8,128)(2,1)S(1)}, u32[]{:S(2)}, u32[]{:S(2)}) async-start(bf16[32,160,128]{2,1,0:T(8,128)(2,1)} %pad_maximum_fusion.1), calls=%async_computation.1 | async-start | bytes 2621440 | tf_op jit(solution)/shard_map/all_to_all | solution.py:50
  142.6 31.2 %all-to-all-done.1 = bf16[32,160,128]{2,1,0:T(8,128)(2,1)S(1)} async-done(((bf16[32,160,128]{2,1,0:T(8,128)(2,1)}), bf16[32,160,128]{2,1,0:T(8,128)(2,1)S(1)}, u32[]{:S(2)}, u32[]{:S(2)}) %all-to-all-start.1) | async-done | bytes 1310752 | tf_op jit(solution)/shard_map/all_to_all | solution.py:50
  175.3 1.3 collective-permute-start.5
  176.8 0.8 collective-permute-done.5
  178.7 43.1 %all_to_all.21 = bf16[32,160,128]{2,1,0:T(8,128)(2,1)S(1)} all-to-all(bf16[32,160,128]{2,1,0:T(8,128)(2,1)S(1)} %bitcast.168), channel_id=1, replica_groups={{0,2,4,6,8,10,12,14,16,18,20,22,24,26,28,30,32,34,36,38,40,42,44,46,48,..., dimensions={0} | all-to-all | bytes 2621440 | tf_op jit(solution)/shard_map/all_to_all | solution.py:50
  222.8 3.3 %fusion.80 = f32[320,768]{1,0:T(8,128)S(1)} fusion(bf16[320,2048]{1,0:T(8,128)(2,1)S(1)} %bitcast_dynamic-update-slice_fusion.1, bf16[2048,768]{1,0:T(8,128)(2,1)} %collective-permute-done.4), kind=kOutput, calls=%fused_computation.155 | convolution fusion | flops 1006632960 | bytes 5439488 | tf_op jit(solution)/shard_map/dot_general | solution.py:75
  226.1 1.2 fusion.68
  227.5 0.9 fusion.33
  228.4 0.9 fusion.1
  229.7 1.2 pad_maximum_fusion.2
  230.9 8.2 %all-to-all-start.3 = ((bf16[32,160,128]{2,1,0:T(8,128)(2,1)}), bf16[32,160,128]{2,1,0:T(8,128)(2,1)S(1)}, u32[]{:S(2)}, u32[]{:S(2)}) async-start(bf16[32,160,128]{2,1,0:T(8,128)(2,1)} %pad_maximum_fusion.2), calls=%async_computation.3 | async-start | bytes 2621440 | tf_op jit(solution)/shard_map/all_to_all | solution.py:50
  239.2 36.4 %all-to-all-done.3 = bf16[32,160,128]{2,1,0:T(8,128)(2,1)S(1)} async-done(((bf16[32,160,128]{2,1,0:T(8,128)(2,1)}), bf16[32,160,128]{2,1,0:T(8,128)(2,1)S(1)}, u32[]{:S(2)}, u32[]{:S(2)}) %all-to-all-start.3) | async-done | bytes 1310752 | tf_op jit(solution)/shard_map/all_to_all | solution.py:50
  276.8 0.7 maximum_bitcast_fusion
  (120 shorter events, 10.1 us)
Async XLA Ops:
  0.0 59.9 %collective-permute-start.3 = (bf16[384,2048]{1,0:T(8,128)(2,1)}, bf16[384,2048]{1,0:T(8,128)(2,1)S(1)}, u32[]{:S(2)}, u32[]{:S(2)}) collective-permute-start(bf16[384,2048]{1,0:T(8,128)(2,1)} %bitcast.197), channel_id=1, source_target_pairs={{0,1},{1,0},{2,3},{3,2},{4,5},{5,4},{6,7},{7,6},{8,9},{9,8},{10,11... | collective-permute-start | bytes 4718600 | tf_op jit(solution)/shard_map/ppermute | solution.py:70
  8.1 47.6 %collective-permute-start = (bf16[32,2176]{1,0:T(8,128)(2,1)S(1)}, bf16[32,2176]{1,0:T(8,128)(2,1)S(1)}, u32[]{:S(2)}, u32[]{:S(2)}) collective-permute-start(bf16[32,2176]{1,0:T(8,128)(2,1)S(1)} %get-tuple-element.16), channel_id=1, source_target_pairs={{0,2},{1,3},{2,4},{3,5},{4,6},{5,7},{6,0},{7,1},{8,10},{9,11},{10,... | collective-permute-start | bytes 417800 | tf_op jit(solution)/shard_map/ppermute | solution.py:58
  14.2 45.5 %collective-permute-start.1 = (bf16[32,2176]{1,0:T(8,128)(2,1)S(1)}, bf16[32,2176]{1,0:T(8,128)(2,1)S(1)}, u32[]{:S(2)}, u32[]{:S(2)}) collective-permute-start(bf16[32,2176]{1,0:T(8,128)(2,1)S(1)} %get-tuple-element.16), channel_id=1, source_target_pairs={{0,4},{1,5},{2,6},{3,7},{4,0},{5,1},{6,2},{7,3},{8,12},{9,13},{10,... | collective-permute-start | bytes 417800 | tf_op jit(solution)/shard_map/ppermute | solution.py:58
  22.5 37.3 %collective-permute-start.2 = (bf16[32,2176]{1,0:T(8,128)(2,1)S(1)}, bf16[32,2176]{1,0:T(8,128)(2,1)S(1)}, u32[]{:S(2)}, u32[]{:S(2)}) collective-permute-start(bf16[32,2176]{1,0:T(8,128)(2,1)S(1)} %get-tuple-element.16), channel_id=1, source_target_pairs={{0,6},{1,7},{2,0},{3,1},{4,2},{5,3},{6,4},{7,5},{8,14},{9,15},{10,... | collective-permute-start | bytes 417800 | tf_op jit(solution)/shard_map/ppermute | solution.py:58
  26.1 92.2 %collective-permute-start.4 = (bf16[2048,768]{1,0:T(8,128)(2,1)}, bf16[2048,768]{1,0:T(8,128)(2,1)}, u32[]{:S(2)}, u32[]{:S(2)}) collective-permute-start(bf16[2048,768]{1,0:T(8,128)(2,1)} %bitcast.196), channel_id=1, source_target_pairs={{0,1},{1,0},{2,3},{3,2},{4,5},{5,4},{6,7},{7,6},{8,9},{9,8},{10,11... | collective-permute-start | bytes 9437192 | tf_op jit(solution)/shard_map/ppermute | solution.py:70
  95.9 22.4 %copy-start.4 = (bf16[1,1,2048,768]{3,2,1,0:T(8,128)(2,1)S(1)}, bf16[1,1,2048,768]{3,2,1,0:T(8,128)(2,1)}, u32[]{:S(2)}) copy-start(bf16[1,1,2048,768]{3,2,1,0:T(8,128)(2,1)} %param.10) | copy-start | bytes 9437188
  119.5 3.2 %copy-start.6 = (bf16[1,1,384,2048]{3,2,1,0:T(8,128)(2,1)S(1)}, bf16[1,1,384,2048]{3,2,1,0:T(8,128)(2,1)}, u32[]{:S(2)}) copy-start(bf16[1,1,384,2048]{3,2,1,0:T(8,128)(2,1)} %param.11) | copy-start | bytes 4718596
  126.1 16.3 %copy-start.3 = (f32[2,1,32,4]{2,3,1,0:T(4,128)S(1)}, f32[2,1,32,4]{2,3,1,0:T(4,128)}, u32[]{:S(2)}) copy-start(f32[2,1,32,4]{2,3,1,0:T(4,128)} %param.13) | copy-start | bytes 3076
  126.1 47.6 %all-to-all-start.1 = ((bf16[32,160,128]{2,1,0:T(8,128)(2,1)}), bf16[32,160,128]{2,1,0:T(8,128)(2,1)S(1)}, u32[]{:S(2)}, u32[]{:S(2)}) async-start(bf16[32,160,128]{2,1,0:T(8,128)(2,1)} %pad_maximum_fusion.1), calls=%async_computation.1 | async-start | bytes 2621440 | tf_op jit(solution)/shard_map/all_to_all | solution.py:50
  174.1 0.9 copy-start
  174.5 3.0 %copy-start.1 = (bf16[1,32,2048]{2,1,0:T(8,128)(2,1)S(1)}, bf16[1,32,2048]{2,1,0:T(8,128)(2,1)}, u32[]{:S(2)}) copy-start(bf16[1,32,2048]{2,1,0:T(8,128)(2,1)} %param.8) | copy-start | bytes 393220
  174.5 3.2 %copy-start.2 = (f32[1,2048]{1,0:T(1,128)S(1)}, f32[1,2048]{1,0:T(1,128)}, u32[]{:S(2)}) copy-start(f32[1,2048]{1,0:T(1,128)} %param.9) | copy-start | bytes 24580
  175.3 2.3 collective-permute-start.5
  222.8 3.3 %copy-start.5 = (bf16[1,1,2048,768]{3,2,1,0:T(8,128)(2,1)S(1)}, bf16[1,1,2048,768]{3,2,1,0:T(8,128)(2,1)}, u32[]{:S(2)}) copy-start(bf16[1,1,2048,768]{3,2,1,0:T(8,128)(2,1)} %param.10) | copy-start | bytes 9437188
  226.1 1.4 copy-start.7
  230.9 44.8 %all-to-all-start.3 = ((bf16[32,160,128]{2,1,0:T(8,128)(2,1)}), bf16[32,160,128]{2,1,0:T(8,128)(2,1)S(1)}, u32[]{:S(2)}, u32[]{:S(2)}) async-start(bf16[32,160,128]{2,1,0:T(8,128)(2,1)} %pad_maximum_fusion.2), calls=%async_computation.3 | async-start | bytes 2621440 | tf_op jit(solution)/shard_map/all_to_all | solution.py:50

commit v5 on v4

--- a/solution.py
+++ b/solution.py
@@ -1,6 +1,8 @@
 import jax
 import jax.numpy as jnp
 from jax import lax
+from jax.experimental import pallas as pl
+from jax.experimental.pallas import tpu as pltpu
 from jax.sharding import PartitionSpec as P
 
 SLICES = 4
@@ -70,10 +72,62 @@
     return lax.ppermute(x, "expert", [(i, i ^ 1) for i in range(length)])
 
 
-def gated(rows, weights):
-    half = weights.shape[1] // 2
-    projected = jnp.dot(rows, weights, preferred_element_type=jnp.float32)
-    return (jax.nn.silu(projected[:, :half]) * projected[:, half:]).astype(jnp.bfloat16)
+def experts_kernel(slices, carried, x_ref, *refs):
+    refs = list(refs)
+    acc_ref = refs.pop(0) if carried else None
+    gate_up = refs[:slices]
+    down = refs[slices:2 * slices]
+    out_ref, gate_up_buffer, down_buffer, total, gate_up_sems, down_sems = refs[2 * slices:]
+    copies = []
+    for i in range(slices):
+        copies.append((
+            pltpu.make_async_copy(gate_up[i], gate_up_buffer.at[i], gate_up_sems.at[i]),
+            pltpu.make_async_copy(down[i], down_buffer.at[i], down_sems.at[i]),
+        ))
+    for first, second in copies:
+        first.start()
+        second.start()
+    half = gate_up_buffer.shape[2] // 2
+    for i, (first, second) in enumerate(copies):
+        first.wait()
+        projected = jnp.dot(x_ref[...], gate_up_buffer[i], preferred_element_type=jnp.float32)
+        hidden = (jax.nn.silu(projected[:, :half]) * projected[:, half:]).astype(jnp.bfloat16)
+        second.wait()
+        value = jnp.dot(hidden, down_buffer[i], preferred_element_type=jnp.float32)
+        if i > 0:
+            value = total[...] + value
+        elif carried:
+            value = acc_ref[...] + value
+        if i + 1 < slices:
+            total[...] = value
+        else:
+            out_ref[...] = value.astype(out_ref.dtype)
+
+
+def experts(rows, gate_up, down, carried=None, dtype=jnp.bfloat16):
+    slices = len(gate_up)
+    count, width = rows.shape
+    out_width = down[0].shape[1]
+    whole = pl.BlockSpec(memory_space=pltpu.VMEM)
+    placed = pl.BlockSpec(memory_space=pl.ANY)
+    operands = [rows] + ([] if carried is None else [carried]) + list(gate_up) + list(down)
+    in_specs = [whole] * (1 if carried is None else 2) + [placed] * (2 * slices)
+    body = lambda *refs: experts_kernel(slices, carried is not None, *refs)
+    return pl.pallas_call(
+        body,
+        out_shape=jax.ShapeDtypeStruct((count, out_width), dtype),
+        in_specs=in_specs,
+        out_specs=whole,
+        scratch_shapes=[
+            pltpu.VMEM((slices,) + gate_up[0].shape, gate_up[0].dtype),
+            pltpu.VMEM((slices,) + down[0].shape, down[0].dtype),
+            pltpu.VMEM((count, out_width), jnp.float32),
+            pltpu.SemaphoreType.DMA((slices,)),
+            pltpu.SemaphoreType.DMA((slices,)),
+        ],
+        compiler_params=pltpu.CompilerParams(vmem_limit_bytes=32 << 20),
+        name=f"experts_{slices}",
+    )(*operands)
 
 
 def first_dispatch(normed, chosen, parts, column, expert_count, swapped_first):
@@ -162,7 +216,9 @@
             at.append(at[-1] + (high - low) * normed.shape[1] // LANES)
         if tick_index == 0:
             rows_in = first_dispatch(normed, routes[0, 0], parts, column, expert_count, down_other)
+            partial_value = experts(rows_in, [gate_up_own], [down_own], dtype=jnp.float32)
             rows_in, gate_up_other = lax.optimization_barrier((rows_in, gate_up_other))
+            partial_value = experts(rows_in, [gate_up_other], [down_other], carried=partial_value)
         else:
             sent = []
             for (low, high), (picker, _, _) in zip(parts, plan):
@@ -171,11 +227,7 @@
             received = exchange(jnp.repeat(jnp.concatenate(sent, axis=1), copies, axis=0))
             rows_in = [from_tiles(received[:, at[i]:at[i + 1]], high - low) for i, (low, high) in enumerate(parts)]
             rows_in = jnp.concatenate(rows_in, axis=0)
-        hidden_own = gated(rows_in, gate_up_own)
-        hidden_other = gated(rows_in, gate_up_other)
-        partial_value = jnp.dot(hidden_own, down_own, preferred_element_type=jnp.float32)
-        partial_value = partial_value + jnp.dot(hidden_other, down_other, preferred_element_type=jnp.float32)
-        partial_value = partial_value.astype(jnp.bfloat16)
+            partial_value = experts(rows_in, [gate_up_own, gate_up_other], [down_own, down_other])
         split = [partial_value[group * low:group * high] for low, high in parts]
         back = exchange(jnp.concatenate([to_tiles(piece, group) for piece in split], axis=1))
         returned = [back[:, at[i]:at[i + 1]] for i in range(len(parts))]

time: 279 us -> 281 us (level); the launches traced: 278 us -> 276 us
  waiting for transfers between devices: 121 us -> 106 us
  Pallas kernels: 0 us -> 11.9 us
  matrix products: 15.2 us -> 4.47 us
  local copies, waits for them, and re-layouts: 6.83 us -> 12.9 us
  other arithmetic: 8.94 us -> 14.8 us
    dot_general x8 -> x0, matrix products: 12.5 us -> none  [the longest x4 8.85 us: gated(): projected = jnp.dot(rows, weights, preferred_element_type=jnp.float32)]
    pallas_call x0 -> x3, Pallas kernels: none -> 11.9 us  [experts(): pl.pallas_call(body, out_shape=jax.ShapeDtypeStruct((count, out_width), d...]
    ppermute x2, waiting for transfers between devices: 22.2 us -> 11.3 us  [swapped(): return lax.ppermute(x, 'expert', [(i, i ^ 1) for i in range(length)])]
    unnamed x24 -> x26, local copies, waits for them, and re-layouts: 1.09 us -> 4.74 us
  transfers between devices with their start and end apart: 8 -> 8, of which waited for: 6 -> 5; matrix products, arithmetic and copies ran while one was open for 4% -> 6% of each run, Pallas kernels for 0% -> 1%
where the time goes in v5:
time: 281 us; the launch traced here: 276 us
  waiting for transfers between devices  106 us (38%)
  blocking collectives  75.2 us (27%)
  starting transfers between devices  49.9 us (18%)
  other arithmetic  14.8 us (5%)
  local copies, waits for them, and re-layouts  12.9 us (5%)
  Pallas kernels  11.9 us (4%)
  matrix products  4.47 us (2%)
    all_to_all x2, waiting for transfers between devices, exchange(): lax.all_to_all(x, 'expert', split_axis=0, concat_axis=0, tiled=True, axis...  64.9 us
    all_to_all x1, blocking collectives, exchange(): lax.all_to_all(x, 'expert', split_axis=0, concat_axis=0, tiled=True, axis...  43.1 us
    all_to_all x1, blocking collectives, exchange_rows(): lax.all_to_all(x, 'expert', split_axis=0, concat_axis=0, tiled=True, axis...  32.1 us
    ppermute x3, waiting for transfers between devices, same_side(): pieces.append(lax.ppermute(x, 'expert', pairs))  30.2 us
    all_to_all x2, starting transfers between devices, exchange(): lax.all_to_all(x, 'expert', split_axis=0, concat_axis=0, tiled=True, axis...  23.3 us
    ppermute x3, starting transfers between devices, same_side(): pieces.append(lax.ppermute(x, 'expert', pairs))  18 us
    pallas_call x3, Pallas kernels, experts(): pl.pallas_call(body, out_shape=jax.ShapeDtypeStruct((count, out_width), d...  11.9 us
    ppermute x2, waiting for transfers between devices, swapped(): return lax.ppermute(x, 'expert', [(i, i ^ 1) for i in range(length)])  11.3 us
  transfers between devices with their start and end apart: 8, of which 5 were waited for; matrix products, arithmetic and copies ran while one was open for 6% of the time, Pallas kernels for 1%

profile of v5, /device:TPU:56, one launch (start us, length us, event | category | flops | bytes accessed | tf_op | source)
XLA Modules:
  0.0 276.3 jit_solution(6027906891616918746)
XLA Ops:
  0.0 4.3 %collective-permute-start.3 = (bf16[384,2048]{1,0:T(8,128)(2,1)}, bf16[384,2048]{1,0:T(8,128)(2,1)}, u32[]{:S(2)}, u32[]{:S(2)}) collective-permute-start(bf16[384,2048]{1,0:T(8,128)(2,1)} %bitcast.152), channel_id=1, source_target_pairs={{0,1},{1,0},{2,3},{3,2},{4,5},{5,4},{6,7},{7,6},{8,9},{9,8},{10,11... | collective-permute-start | bytes 4718600 | tf_op jit(solution)/shard_map/ppermute | solution.py:72
  6.0 1.0 fusion.21
  7.1 1.0 fusion.23
  8.8 6.1 %collective-permute-start = (bf16[32,2176]{1,0:T(8,128)(2,1)}, bf16[32,2176]{1,0:T(8,128)(2,1)S(1)}, u32[]{:S(2)}, u32[]{:S(2)}) collective-permute-start(bf16[32,2176]{1,0:T(8,128)(2,1)} %get-tuple-element.16), channel_id=1, source_target_pairs={{0,2},{1,3},{2,4},{3,5},{4,6},{5,7},{6,0},{7,1},{8,10},{9,11},{10,... | collective-permute-start | bytes 417800 | tf_op jit(solution)/shard_map/ppermute | solution.py:60
  14.9 8.2 %collective-permute-start.1 = (bf16[32,2176]{1,0:T(8,128)(2,1)}, bf16[32,2176]{1,0:T(8,128)(2,1)}, u32[]{:S(2)}, u32[]{:S(2)}) collective-permute-start(bf16[32,2176]{1,0:T(8,128)(2,1)} %get-tuple-element.16), channel_id=1, source_target_pairs={{0,4},{1,5},{2,6},{3,7},{4,0},{5,1},{6,2},{7,3},{8,12},{9,13},{10,... | collective-permute-start | bytes 417800 | tf_op jit(solution)/shard_map/ppermute | solution.py:60
  23.1 3.7 %collective-permute-start.2 = (bf16[32,2176]{1,0:T(8,128)(2,1)}, bf16[32,2176]{1,0:T(8,128)(2,1)}, u32[]{:S(2)}, u32[]{:S(2)}) collective-permute-start(bf16[32,2176]{1,0:T(8,128)(2,1)} %get-tuple-element.16), channel_id=1, source_target_pairs={{0,6},{1,7},{2,0},{3,1},{4,2},{5,3},{6,4},{7,5},{8,14},{9,15},{10,... | collective-permute-start | bytes 417800 | tf_op jit(solution)/shard_map/ppermute | solution.py:60
  26.8 2.5 collective-permute-start.4
  29.7 26.0 %collective-permute-done = bf16[32,2176]{1,0:T(8,128)(2,1)S(1)} collective-permute-done((bf16[32,2176]{1,0:T(8,128)(2,1)}, bf16[32,2176]{1,0:T(8,128)(2,1)S(1)}, u32[]{:S(2)}, u32[]{:S(2)}) %collective-permute-start) | collective-permute-done | bytes 139296 | tf_op jit(solution)/shard_map/ppermute | solution.py:60
  55.7 4.1 %collective-permute-done.1 = bf16[32,2176]{1,0:T(8,128)(2,1)} collective-permute-done((bf16[32,2176]{1,0:T(8,128)(2,1)}, bf16[32,2176]{1,0:T(8,128)(2,1)}, u32[]{:S(2)}, u32[]{:S(2)}) %collective-permute-start.1) | collective-permute-done | bytes 139296 | tf_op jit(solution)/shard_map/ppermute | solution.py:60
  59.9 1.9 pad_maximum_fusion.5
  61.8 2.7 copy.205
  64.5 1.9 slice.58
  67.9 1.5 convolution_convert_fusion
  69.4 32.1 %all_to_all.20 = bf16[8,40,2048]{2,1,0:T(8,128)(2,1)S(1)} all-to-all(bf16[8,40,2048]{2,1,0:T(8,128)(2,1)S(1)} %bitcast.155), channel_id=1, replica_groups={{0,8,16,24,32,40,48,56},{1,9,17,25,33,41,49,57},{2,10,18,26,34,42,50,58..., dimensions={0} | all-to-all | bytes 2621440 | tf_op jit(solution)/shard_map/all_to_all | solution.py:67
  101.7 1.2 copy-done.2
  102.9 1.0 copy-done
  103.9 3.0 %experts_1.2.refs_1_ = f32[320,2048]{1,0:T(8,128)S(1)} custom-call(bf16[320,2048]{1,0:T(8,128)(2,1)S(1)} %pad_maximum_fusion.refs_0_, bf16[2048,768]{1,0:T(8,128)(2,1)S(1)} %bitcast.150, bf16[384,2048]{1,0:T(8,128)(2,1)S(1)} %bitcast.153), custom_call_target="tpu_custom_call" | custom-call | tf_op jit(solution)/shard_map/experts_1/pallas_call | solution.py:116
  106.9 11.3 %collective-permute-done.4.refs_2_ = bf16[2048,768]{1,0:T(8,128)(2,1)S(1)} collective-permute-done((bf16[2048,768]{1,0:T(8,128)(2,1)}, bf16[2048,768]{1,0:T(8,128)(2,1)S(1)}, u32[]{:S(2)}, u32[]{:S(2)}) %collective-permute-start.4) | collective-permute-done | bytes 3145760 | tf_op jit(solution)/shard_map/ppermute | solution.py:72
  118.2 2.9 %experts_1.3 = bf16[320,2048]{1,0:T(8,128)(2,1)S(1)} custom-call(bf16[320,2048]{1,0:T(8,128)(2,1)S(1)} %pad_maximum_fusion.refs_0_, f32[320,2048]{1,0:T(8,128)S(1)} %experts_1.2.refs_1_, bf16[2048,768]{1,0:T(8,128)(2,1)S(1)} %collective-permute-done.4.refs_2_, bf16[384,2048]{1,0:T(8,128)(2,1)} %collective-permute-done.3.refs_3_.refs_4_), custom_call_target="tpu_custom_call" | custom-call | tf_op jit(solution)/shard_map/experts_1/pallas_call | solution.py:116
  121.5 1.2 pad_maximum_fusion.1
  122.7 15.1 %all-to-all-start.1 = ((bf16[32,160,128]{2,1,0:T(8,128)(2,1)}), bf16[32,160,128]{2,1,0:T(8,128)(2,1)}, u32[]{:S(2)}, u32[]{:S(2)}) async-start(bf16[32,160,128]{2,1,0:T(8,128)(2,1)} %pad_maximum_fusion.1), calls=%async_computation.1 | async-start | bytes 2621440 | tf_op jit(solution)/shard_map/all_to_all | solution.py:52
  139.7 30.7 %all-to-all-done.1 = bf16[32,160,128]{2,1,0:T(8,128)(2,1)} async-done(((bf16[32,160,128]{2,1,0:T(8,128)(2,1)}), bf16[32,160,128]{2,1,0:T(8,128)(2,1)}, u32[]{:S(2)}, u32[]{:S(2)}) %all-to-all-start.1) | async-done | bytes 1310752 | tf_op jit(solution)/shard_map/all_to_all | solution.py:52
  170.4 1.0 bitcast_reduce_fusion.3
  171.9 1.4 bitcast_reduce_fusion.1
  173.8 1.9 collective-permute-start.5
  177.1 0.9 fusion.10
  178.4 43.1 %all_to_all.21 = bf16[32,160,128]{2,1,0:T(8,128)(2,1)S(1)} all-to-all(bf16[32,160,128]{2,1,0:T(8,128)(2,1)S(1)} %bitcast.156), channel_id=1, replica_groups={{0,2,4,6,8,10,12,14,16,18,20,22,24,26,28,30,32,34,36,38,40,42,44,46,48,..., dimensions={0} | all-to-all | bytes 2621440 | tf_op jit(solution)/shard_map/all_to_all | solution.py:52
  222.2 1.6 copy-done.1
  224.3 5.9 %experts_2.1 = bf16[320,2048]{1,0:T(8,128)(2,1)S(1)} custom-call(bf16[320,2048]{1,0:T(8,128)(2,1)S(1)} %pad_maximum_fusion.2.refs_0_, bf16[2048,768]{1,0:T(8,128)(2,1)S(1)} %bitcast.151, bf16[2048,768]{1,0:T(8,128)(2,1)S(1)} %collective-permute-done.4.refs_2_, bf16[384,2048]{1,0:T(8,128)(2,1)S(1)} %bitcast.154, ...), custom_call_target="tpu_custom_call" | custom-call | tf_op jit(solution)/shard_map/experts_2/pallas_call | solution.py:116
  230.6 1.2 pad_maximum_fusion.3
  231.8 8.2 %all-to-all-start.3 = ((bf16[32,160,128]{2,1,0:T(8,128)(2,1)}), bf16[32,160,128]{2,1,0:T(8,128)(2,1)S(1)}, u32[]{:S(2)}, u32[]{:S(2)}) async-start(bf16[32,160,128]{2,1,0:T(8,128)(2,1)} %pad_maximum_fusion.3), calls=%async_computation.3 | async-start | bytes 2621440 | tf_op jit(solution)/shard_map/all_to_all | solution.py:52
  240.2 34.2 %all-to-all-done.3 = bf16[32,160,128]{2,1,0:T(8,128)(2,1)S(1)} async-done(((bf16[32,160,128]{2,1,0:T(8,128)(2,1)}), bf16[32,160,128]{2,1,0:T(8,128)(2,1)S(1)}, u32[]{:S(2)}, u32[]{:S(2)}) %all-to-all-start.3) | async-done | bytes 1310752 | tf_op jit(solution)/shard_map/all_to_all | solution.py:52
  (116 shorter events, 12.6 us)
Async XLA Ops:
  0.0 61.8 %collective-permute-start.3 = (bf16[384,2048]{1,0:T(8,128)(2,1)}, bf16[384,2048]{1,0:T(8,128)(2,1)}, u32[]{:S(2)}, u32[]{:S(2)}) collective-permute-start(bf16[384,2048]{1,0:T(8,128)(2,1)} %bitcast.152), channel_id=1, source_target_pairs={{0,1},{1,0},{2,3},{3,2},{4,5},{5,4},{6,7},{7,6},{8,9},{9,8},{10,11... | collective-permute-start | bytes 4718600 | tf_op jit(solution)/shard_map/ppermute | solution.py:72
  8.8 46.9 %collective-permute-start = (bf16[32,2176]{1,0:T(8,128)(2,1)}, bf16[32,2176]{1,0:T(8,128)(2,1)S(1)}, u32[]{:S(2)}, u32[]{:S(2)}) collective-permute-start(bf16[32,2176]{1,0:T(8,128)(2,1)} %get-tuple-element.16), channel_id=1, source_target_pairs={{0,2},{1,3},{2,4},{3,5},{4,6},{5,7},{6,0},{7,1},{8,10},{9,11},{10,... | collective-permute-start | bytes 417800 | tf_op jit(solution)/shard_map/ppermute | solution.py:60
  14.9 45.0 %collective-permute-start.1 = (bf16[32,2176]{1,0:T(8,128)(2,1)}, bf16[32,2176]{1,0:T(8,128)(2,1)}, u32[]{:S(2)}, u32[]{:S(2)}) collective-permute-start(bf16[32,2176]{1,0:T(8,128)(2,1)} %get-tuple-element.16), channel_id=1, source_target_pairs={{0,4},{1,5},{2,6},{3,7},{4,0},{5,1},{6,2},{7,3},{8,12},{9,13},{10,... | collective-permute-start | bytes 417800 | tf_op jit(solution)/shard_map/ppermute | solution.py:60
  23.1 36.8 %collective-permute-start.2 = (bf16[32,2176]{1,0:T(8,128)(2,1)}, bf16[32,2176]{1,0:T(8,128)(2,1)}, u32[]{:S(2)}, u32[]{:S(2)}) collective-permute-start(bf16[32,2176]{1,0:T(8,128)(2,1)} %get-tuple-element.16), channel_id=1, source_target_pairs={{0,6},{1,7},{2,0},{3,1},{4,2},{5,3},{6,4},{7,5},{8,14},{9,15},{10,... | collective-permute-start | bytes 417800 | tf_op jit(solution)/shard_map/ppermute | solution.py:60
  26.8 91.4 %collective-permute-start.4 = (bf16[2048,768]{1,0:T(8,128)(2,1)}, bf16[2048,768]{1,0:T(8,128)(2,1)S(1)}, u32[]{:S(2)}, u32[]{:S(2)}) collective-permute-start(bf16[2048,768]{1,0:T(8,128)(2,1)} %bitcast.149), channel_id=1, source_target_pairs={{0,1},{1,0},{2,3},{3,2},{4,5},{5,4},{6,7},{7,6},{8,9},{9,8},{10,11... | collective-permute-start | bytes 9437192 | tf_op jit(solution)/shard_map/ppermute | solution.py:72
  101.5 1.4 copy-start.2
  101.6 2.3 copy-start
  122.7 16.3 %copy-start.8 = (f32[2,1,32,4]{2,3,1,0:T(4,128)S(1)}, f32[2,1,32,4]{2,3,1,0:T(4,128)}, u32[]{:S(2)}) copy-start(f32[2,1,32,4]{2,3,1,0:T(4,128)} %param.13) | copy-start | bytes 3076
  122.7 47.7 %all-to-all-start.1 = ((bf16[32,160,128]{2,1,0:T(8,128)(2,1)}), bf16[32,160,128]{2,1,0:T(8,128)(2,1)}, u32[]{:S(2)}, u32[]{:S(2)}) async-start(bf16[32,160,128]{2,1,0:T(8,128)(2,1)} %pad_maximum_fusion.1), calls=%async_computation.1 | async-start | bytes 2621440 | tf_op jit(solution)/shard_map/all_to_all | solution.py:52
  171.7 1.8 copy-start.4
  173.3 3.2 %copy-start.5 = (bf16[1,32,2048]{2,1,0:T(8,128)(2,1)S(1)}, bf16[1,32,2048]{2,1,0:T(8,128)(2,1)}, u32[]{:S(2)}) copy-start(bf16[1,32,2048]{2,1,0:T(8,128)(2,1)} %param.8) | copy-start | bytes 393220
  173.4 3.4 %copy-start.6 = (f32[1,2048]{1,0:T(1,128)S(1)}, f32[1,2048]{1,0:T(1,128)}, u32[]{:S(2)}) copy-start(f32[1,2048]{1,0:T(1,128)} %param.9) | copy-start | bytes 24580
  173.8 2.7 collective-permute-start.5
  222.0 1.9 copy-start.1
  222.1 2.2 copy-start.3
  231.8 8.2 %copy-start.7 = (f32[32,4]{0,1:T(4,128)S(1)}, f32[32,4]{0,1:T(4,128)}, u32[]{:S(2)}) copy-start(f32[32,4]{0,1:T(4,128)} %get-tuple-element.22) | copy-start | bytes 1540
  231.8 42.6 %all-to-all-start.3 = ((bf16[32,160,128]{2,1,0:T(8,128)(2,1)}), bf16[32,160,128]{2,1,0:T(8,128)(2,1)S(1)}, u32[]{:S(2)}, u32[]{:S(2)}) async-start(bf16[32,160,128]{2,1,0:T(8,128)(2,1)} %pad_maximum_fusion.3), calls=%async_computation.3 | async-start | bytes 2621440 | tf_op jit(solution)/shard_map/all_to_all | solution.py:52

commit v6 on v4

--- a/solution.py
+++ b/solution.py
@@ -8,6 +8,8 @@
 TICKS = 2
 LANES = 128
 ROWS = 8
+FAR = (3, 6, 5, 0, 7, 2, 1, 4)
+NEAR = (7, 2, 1, 4, 3, 6, 5, 0)
 COLUMNS = 8
 SHARE = 2
 
@@ -44,19 +46,24 @@
     return jnp.sum((jnp.cumsum(onehot, axis=0) - onehot) * onehot, axis=1)
 
 
+def side_of(column):
+    return (column ^ (column >> 1)) % SHARE
+
+
 def exchange(x):
     length = lax.axis_size("expert")
-    groups = [list(range(first, length, SHARE)) for first in range(SHARE)]
+    groups = [[i for i in range(length) if side_of(i % COLUMNS) == side] for side in range(SHARE)]
     return lax.all_to_all(x, "expert", split_axis=0, concat_axis=0, tiled=True, axis_index_groups=groups)
 
 
+def within_row(x, targets):
+    length = lax.axis_size("expert")
+    return lax.ppermute(x, "expert", [(i, i // COLUMNS * COLUMNS + targets[i % COLUMNS]) for i in range(length)])
+
+
 def same_side(x):
-    length = lax.axis_size("expert")
-    pieces = [x]
-    for by in range(SHARE, COLUMNS, SHARE):
-        pairs = [(i, i // COLUMNS * COLUMNS + (i + by) % COLUMNS) for i in range(length)]
-        pieces.append(lax.ppermute(x, "expert", pairs))
-    return jnp.stack(pieces)
+    pair = jnp.stack([x, within_row(x, FAR)])
+    return jnp.concatenate([pair, within_row(pair, NEAR)], axis=0)
 
 
 def exchange_rows(x):
@@ -87,8 +94,8 @@
     slot_at = jnp.pad(slot_at, ((0, 0), (0, LANES - expert_count))).astype(jnp.bfloat16)
     everyone = same_side(jnp.concatenate([normed, slot_at], axis=1))
     everyone, _ = lax.optimization_barrier((everyone, swapped_first))
-    mine = column // SHARE
-    position = (mine - jnp.arange(sources, dtype=jnp.int32)) % sources
+    arrivals = [[z, FAR[z], NEAR[z], FAR[NEAR[z]]] for z in range(COLUMNS)]
+    position = jnp.asarray(arrivals, dtype=jnp.int32)[column] // SHARE
     origin = jnp.arange(sources, dtype=jnp.int32)[:, None] == position[None, :]
     slots = everyone[:, :, width:width + expert_count].astype(jnp.int32) - 1
     slots = slots.reshape(sources, tokens, rows_of_chips, halves)

time: 279 us -> 274 us (0.982)
  the two profiles are of different devices: /device:TPU:56 before, /device:TPU:82 now
where the time goes in v6:
time: 274 us
  waiting for transfers between devices  123 us (45%)
  blocking collectives  77.5 us (28%)
  starting transfers between devices  40.1 us (15%)
  matrix products  15.2 us (6%)
  other arithmetic  9.66 us (4%)
  local copies, waits for them, and re-layouts  6.81 us (2%)
    all_to_all x2, waiting for transfers between devices, exchange(): lax.all_to_all(x, 'expert', split_axis=0, concat_axis=0, tiled=True, axis...  69.2 us
    all_to_all x1, blocking collectives, exchange(): lax.all_to_all(x, 'expert', split_axis=0, concat_axis=0, tiled=True, axis...  42.4 us
    ppermute x2, waiting for transfers between devices, within_row(): lax.ppermute(x, 'expert', [(i, i // COLUMNS * COLUMNS + targets[i % COLUM...  39.1 us
    all_to_all x1, blocking collectives, exchange_rows(): lax.all_to_all(x, 'expert', split_axis=0, concat_axis=0, tiled=True, axis...  35.1 us
    all_to_all x2, starting transfers between devices, exchange(): lax.all_to_all(x, 'expert', split_axis=0, concat_axis=0, tiled=True, axis...  21 us
    ppermute x2, starting transfers between devices, within_row(): lax.ppermute(x, 'expert', [(i, i // COLUMNS * COLUMNS + targets[i % COLUM...  13.4 us
    ppermute x2, waiting for transfers between devices, swapped(): return lax.ppermute(x, 'expert', [(i, i ^ 1) for i in range(length)])  11 us
    dot_general x4, matrix products, gated(): projected = jnp.dot(rows, weights, preferred_element_type=jnp.float32)  8.84 us
  transfers between devices with their start and end apart: 7, of which 6 were waited for; matrix products, arithmetic and copies ran while one was open for 4% of the time, Pallas kernels for 0%

profile of v6, /device:TPU:82, one launch (start us, length us, event | category | flops | bytes accessed | tf_op | source)
XLA Modules:
  0.0 273.5 jit_solution(8642024159166868584)
XLA Ops:
  0.0 1.9 collective-permute-start.2
  1.9 0.7 multiply_bitcast_fusion.1
  3.7 1.0 fusion.27
  4.7 1.0 fusion.29
  5.8 11.5 %collective-permute-start = (bf16[32,2176]{1,0:T(8,128)(2,1)S(1)}, bf16[32,2176]{1,0:T(8,128)(2,1)S(1)}, u32[]{:S(2)}, u32[]{:S(2)}) collective-permute-start(bf16[32,2176]{1,0:T(8,128)(2,1)S(1)} %get-tuple-element.16), channel_id=1, source_target_pairs={{0,3},{1,6},{2,5},{3,0},{4,7},{5,2},{6,1},{7,4},{8,11},{9,14},{10,... | collective-permute-start | bytes 417800 | tf_op jit(solution)/shard_map/ppermute | solution.py:61
  17.3 1.9 collective-permute-start.3
  19.2 0.7 fusion.67
  19.9 33.0 %collective-permute-done = bf16[32,2176]{1,0:T(8,128)(2,1)S(1)} collective-permute-done((bf16[32,2176]{1,0:T(8,128)(2,1)S(1)}, bf16[32,2176]{1,0:T(8,128)(2,1)S(1)}, u32[]{:S(2)}, u32[]{:S(2)}) %collective-permute-start) | collective-permute-done | bytes 139296 | tf_op jit(solution)/shard_map/ppermute | solution.py:61
  53.0 1.9 collective-permute-start.1
  55.3 6.1 %collective-permute-done.1 = bf16[2,32,2176]{2,1,0:T(8,128)(2,1)S(1)} collective-permute-done((bf16[2,32,2176]{2,1,0:T(8,128)(2,1)S(1)}, bf16[2,32,2176]{2,1,0:T(8,128)(2,1)S(1)}, u32[]{:S(2)}, u32[]{:S(2)}) %collective-permute-start.1) | collective-permute-done | bytes 278560 | tf_op jit(solution)/shard_map/ppermute | solution.py:61
  61.5 1.8 copy.232
  63.4 0.7 convert_add_fusion
  65.4 35.1 %all_to_all.20 = bf16[8,40,2048]{2,1,0:T(8,128)(2,1)S(1)} all-to-all(bf16[8,40,2048]{2,1,0:T(8,128)(2,1)S(1)} %bitcast.167), channel_id=1, replica_groups={{0,8,16,24,32,40,48,56},{1,9,17,25,33,41,49,57},{2,10,18,26,34,42,50,58..., dimensions={0} | all-to-all | bytes 2621440 | tf_op jit(solution)/shard_map/all_to_all | solution.py:72
  100.7 11.0 %collective-permute-done.3 = bf16[2048,768]{1,0:T(8,128)(2,1)} collective-permute-done((bf16[2048,768]{1,0:T(8,128)(2,1)}, bf16[2048,768]{1,0:T(8,128)(2,1)}, u32[]{:S(2)}, u32[]{:S(2)}) %collective-permute-start.3) | collective-permute-done | bytes 3145760 | tf_op jit(solution)/shard_map/ppermute | solution.py:77
  111.7 1.2 fusion.70
  112.9 3.2 %fusion.79 = f32[320,768]{1,0:T(8,128)S(1)} fusion(bf16[320,2048]{1,0:T(8,128)(2,1)S(1)} %pad_maximum_fusion, bf16[2048,768]{1,0:T(8,128)(2,1)} %collective-permute-done.3), kind=kOutput, calls=%fused_computation.156 | convolution fusion | flops 1006632960 | bytes 5439488 | tf_op jit(solution)/shard_map/dot_general | solution.py:82
  116.1 0.9 fusion.30
  117.0 0.9 fusion
  118.3 1.2 pad_maximum_fusion.1
  119.5 15.3 %all-to-all-start.1 = ((bf16[32,160,128]{2,1,0:T(8,128)(2,1)}), bf16[32,160,128]{2,1,0:T(8,128)(2,1)S(1)}, u32[]{:S(2)}, u32[]{:S(2)}) async-start(bf16[32,160,128]{2,1,0:T(8,128)(2,1)} %pad_maximum_fusion.1), calls=%async_computation.1 | async-start | bytes 2621440 | tf_op jit(solution)/shard_map/all_to_all | solution.py:56
  136.2 33.6 %all-to-all-done.1 = bf16[32,160,128]{2,1,0:T(8,128)(2,1)S(1)} async-done(((bf16[32,160,128]{2,1,0:T(8,128)(2,1)}), bf16[32,160,128]{2,1,0:T(8,128)(2,1)S(1)}, u32[]{:S(2)}, u32[]{:S(2)}) %all-to-all-start.1) | async-done | bytes 1310752 | tf_op jit(solution)/shard_map/all_to_all | solution.py:56
  171.2 1.9 collective-permute-start.4
  173.4 4.2 %collective-permute-done.4 = bf16[32,2048]{1,0:T(8,128)(2,1)S(1)} collective-permute-done((bf16[32,2048]{1,0:T(8,128)(2,1)S(1)}, bf16[32,2048]{1,0:T(8,128)(2,1)S(1)}, u32[]{:S(2)}, u32[]{:S(2)}) %collective-permute-start.4) | collective-permute-done | bytes 131104 | tf_op jit(solution)/shard_map/ppermute | solution.py:23
  178.7 42.4 %all_to_all.21 = bf16[32,160,128]{2,1,0:T(8,128)(2,1)S(1)} all-to-all(bf16[32,160,128]{2,1,0:T(8,128)(2,1)S(1)} %bitcast.168), channel_id=1, replica_groups={{0,3,4,7,8,11,12,15,16,19,20,23,24,27,28,31,32,35,36,39,40,43,44,47,48,..., dimensions={0} | all-to-all | bytes 2621440 | tf_op jit(solution)/shard_map/all_to_all | solution.py:56
  222.1 3.3 %fusion.80 = f32[320,768]{1,0:T(8,128)S(1)} fusion(bf16[320,2048]{1,0:T(8,128)(2,1)S(1)} %bitcast_dynamic-update-slice_fusion.1, bf16[2048,768]{1,0:T(8,128)(2,1)} %collective-permute-done.3), kind=kOutput, calls=%fused_computation.157 | convolution fusion | flops 1006632960 | bytes 5439488 | tf_op jit(solution)/shard_map/dot_general | solution.py:82
  225.4 1.2 fusion.68
  226.8 0.9 fusion.33
  227.7 0.9 fusion.1
  229.0 1.2 pad_maximum_fusion.2
  230.1 5.7 %all-to-all-start.3 = ((bf16[32,160,128]{2,1,0:T(8,128)(2,1)}), bf16[32,160,128]{2,1,0:T(8,128)(2,1)S(1)}, u32[]{:S(2)}, u32[]{:S(2)}) async-start(bf16[32,160,128]{2,1,0:T(8,128)(2,1)} %pad_maximum_fusion.2), calls=%async_computation.3 | async-start | bytes 2621440 | tf_op jit(solution)/shard_map/all_to_all | solution.py:56
  236.0 35.7 %all-to-all-done.3 = bf16[32,160,128]{2,1,0:T(8,128)(2,1)S(1)} async-done(((bf16[32,160,128]{2,1,0:T(8,128)(2,1)}), bf16[32,160,128]{2,1,0:T(8,128)(2,1)S(1)}, u32[]{:S(2)}, u32[]{:S(2)}) %all-to-all-start.3) | async-done | bytes 1310752 | tf_op jit(solution)/shard_map/all_to_all | solution.py:56
  272.8 0.7 maximum_bitcast_fusion
  (119 shorter events, 10.1 us)
Async XLA Ops:
  0.0 61.5 %collective-permute-start.2 = (bf16[384,2048]{1,0:T(8,128)(2,1)}, bf16[384,2048]{1,0:T(8,128)(2,1)S(1)}, u32[]{:S(2)}, u32[]{:S(2)}) collective-permute-start(bf16[384,2048]{1,0:T(8,128)(2,1)} %bitcast.196), channel_id=1, source_target_pairs={{0,1},{1,0},{2,3},{3,2},{4,5},{5,4},{6,7},{7,6},{8,9},{9,8},{10,11... | collective-permute-start | bytes 4718600 | tf_op jit(solution)/shard_map/ppermute | solution.py:77
  5.8 47.1 %collective-permute-start = (bf16[32,2176]{1,0:T(8,128)(2,1)S(1)}, bf16[32,2176]{1,0:T(8,128)(2,1)S(1)}, u32[]{:S(2)}, u32[]{:S(2)}) collective-permute-start(bf16[32,2176]{1,0:T(8,128)(2,1)S(1)} %get-tuple-element.16), channel_id=1, source_target_pairs={{0,3},{1,6},{2,5},{3,0},{4,7},{5,2},{6,1},{7,4},{8,11},{9,14},{10,... | collective-permute-start | bytes 417800 | tf_op jit(solution)/shard_map/ppermute | solution.py:61
  17.3 94.4 %collective-permute-start.3 = (bf16[2048,768]{1,0:T(8,128)(2,1)}, bf16[2048,768]{1,0:T(8,128)(2,1)}, u32[]{:S(2)}, u32[]{:S(2)}) collective-permute-start(bf16[2048,768]{1,0:T(8,128)(2,1)} %bitcast.195), channel_id=1, source_target_pairs={{0,1},{1,0},{2,3},{3,2},{4,5},{5,4},{6,7},{7,6},{8,9},{9,8},{10,11... | collective-permute-start | bytes 9437192 | tf_op jit(solution)/shard_map/ppermute | solution.py:77
  53.0 8.4 %collective-permute-start.1 = (bf16[2,32,2176]{2,1,0:T(8,128)(2,1)S(1)}, bf16[2,32,2176]{2,1,0:T(8,128)(2,1)S(1)}, u32[]{:S(2)}, u32[]{:S(2)}) collective-permute-start(bf16[2,32,2176]{2,1,0:T(8,128)(2,1)S(1)} %pad_maximum_fusion.5), channel_id=1, source_target_pairs={{0,7},{1,2},{2,1},{3,4},{4,3},{5,6},{6,5},{7,0},{8,15},{9,10},{10,... | collective-permute-start | bytes 835592 | tf_op jit(solution)/shard_map/ppermute | solution.py:61
  100.6 11.2 %copy-start.4 = (bf16[1,1,2048,768]{3,2,1,0:T(8,128)(2,1)S(1)}, bf16[1,1,2048,768]{3,2,1,0:T(8,128)(2,1)}, u32[]{:S(2)}) copy-start(bf16[1,1,2048,768]{3,2,1,0:T(8,128)(2,1)} %param.11) | copy-start | bytes 9437188
  112.9 3.2 %copy-start.6 = (bf16[1,1,384,2048]{3,2,1,0:T(8,128)(2,1)S(1)}, bf16[1,1,384,2048]{3,2,1,0:T(8,128)(2,1)}, u32[]{:S(2)}) copy-start(bf16[1,1,384,2048]{3,2,1,0:T(8,128)(2,1)} %param.12) | copy-start | bytes 4718596
  119.5 16.5 %copy-start.3 = (f32[2,1,32,4]{2,3,1,0:T(4,128)S(1)}, f32[2,1,32,4]{2,3,1,0:T(4,128)}, u32[]{:S(2)}) copy-start(f32[2,1,32,4]{2,3,1,0:T(4,128)} %param.14) | copy-start | bytes 3076
  119.5 50.2 %all-to-all-start.1 = ((bf16[32,160,128]{2,1,0:T(8,128)(2,1)}), bf16[32,160,128]{2,1,0:T(8,128)(2,1)S(1)}, u32[]{:S(2)}, u32[]{:S(2)}) async-start(bf16[32,160,128]{2,1,0:T(8,128)(2,1)} %pad_maximum_fusion.1), calls=%async_computation.1 | async-start | bytes 2621440 | tf_op jit(solution)/shard_map/all_to_all | solution.py:56
  170.1 0.9 copy-start
  170.5 7.0 %copy-start.1 = (bf16[1,32,2048]{2,1,0:T(8,128)(2,1)S(1)}, bf16[1,32,2048]{2,1,0:T(8,128)(2,1)}, u32[]{:S(2)}) copy-start(bf16[1,32,2048]{2,1,0:T(8,128)(2,1)} %param.9) | copy-start | bytes 393220
  170.5 7.2 %copy-start.2 = (f32[1,2048]{1,0:T(1,128)S(1)}, f32[1,2048]{1,0:T(1,128)}, u32[]{:S(2)}) copy-start(f32[1,2048]{1,0:T(1,128)} %param.10) | copy-start | bytes 24580
  171.2 6.3 %collective-permute-start.4 = (bf16[32,2048]{1,0:T(8,128)(2,1)S(1)}, bf16[32,2048]{1,0:T(8,128)(2,1)S(1)}, u32[]{:S(2)}, u32[]{:S(2)}) collective-permute-start(bf16[32,2048]{1,0:T(8,128)(2,1)S(1)} %fusion.9), channel_id=1, source_target_pairs={{0,64},{64,128},{128,192},{192,256},{256,320},{320,384},{384,448},... | collective-permute-start | bytes 393224 | tf_op jit(solution)/shard_map/ppermute | solution.py:23
  222.1 3.3 %copy-start.5 = (bf16[1,1,2048,768]{3,2,1,0:T(8,128)(2,1)S(1)}, bf16[1,1,2048,768]{3,2,1,0:T(8,128)(2,1)}, u32[]{:S(2)}) copy-start(bf16[1,1,2048,768]{3,2,1,0:T(8,128)(2,1)} %param.11) | copy-start | bytes 9437188
  225.4 1.4 copy-start.7
  230.1 41.5 %all-to-all-start.3 = ((bf16[32,160,128]{2,1,0:T(8,128)(2,1)}), bf16[32,160,128]{2,1,0:T(8,128)(2,1)S(1)}, u32[]{:S(2)}, u32[]{:S(2)}) async-start(bf16[32,160,128]{2,1,0:T(8,128)(2,1)} %pad_maximum_fusion.2), calls=%async_computation.3 | async-start | bytes 2621440 | tf_op jit(solution)/shard_map/all_to_all | solution.py:56

commit v7 on v6

--- a/solution.py
+++ b/solution.py
@@ -137,7 +137,11 @@
     column = lax.axis_index("expert") % COLUMNS
     section_index = lax.axis_index("section")
     gate_up_own, down_own = w_gate_up[0, 0], w_down[0, 0]
-    down_other = swapped(down_own)
+    early = down_own.shape[0] * 5 // 6
+    down_early = down_own[:early]
+    states, down_early = lax.optimization_barrier((states, down_early))
+    down_early = swapped(down_early)
+    down_late = swapped(down_own[early:])
     gate_up_other = swapped(gate_up_own)
     gain_values = norm_gain[0]
     plans = []
@@ -168,7 +172,7 @@
         for low, high in parts:
             at.append(at[-1] + (high - low) * normed.shape[1] // LANES)
         if tick_index == 0:
-            rows_in = first_dispatch(normed, routes[0, 0], parts, column, expert_count, down_other)
+            rows_in = first_dispatch(normed, routes[0, 0], parts, column, expert_count, down_early)
             rows_in, gate_up_other = lax.optimization_barrier((rows_in, gate_up_other))
         else:
             sent = []
@@ -181,7 +185,8 @@
         hidden_own = gated(rows_in, gate_up_own)
         hidden_other = gated(rows_in, gate_up_other)
         partial_value = jnp.dot(hidden_own, down_own, preferred_element_type=jnp.float32)
-        partial_value = partial_value + jnp.dot(hidden_other, down_other, preferred_element_type=jnp.float32)
+        partial_value = partial_value + jnp.dot(hidden_other[:, :early], down_early, preferred_element_type=jnp.float32)
+        partial_value = partial_value + jnp.dot(hidden_other[:, early:], down_late, preferred_element_type=jnp.float32)
         partial_value = partial_value.astype(jnp.bfloat16)
         split = [partial_value[group * low:group * high] for low, high in parts]
         back = exchange(jnp.concatenate([to_tiles(piece, group) for piece in split], axis=1))

time: 274 us -> 271 us (0.989)
  the two profiles are of different devices: /device:TPU:82 before, /device:TPU:84 now
where the time goes in v7:
time: 271 us; the launch traced here: 270 us
  waiting for transfers between devices  144 us (53%)
  starting transfers between devices  49.6 us (18%)
  blocking collectives  41.6 us (15%)
  matrix products  17.3 us (6%)
  local copies, waits for them, and re-layouts  9.91 us (4%)
  other arithmetic  7.44 us (3%)
    all_to_all x2, waiting for transfers between devices, exchange(): lax.all_to_all(x, 'expert', split_axis=0, concat_axis=0, tiled=True, axis...  67.8 us
    all_to_all x1, blocking collectives, exchange(): lax.all_to_all(x, 'expert', split_axis=0, concat_axis=0, tiled=True, axis...  41.6 us
    ppermute x2, waiting for transfers between devices, within_row(): lax.ppermute(x, 'expert', [(i, i // COLUMNS * COLUMNS + targets[i % COLUM...  36 us
    all_to_all x1, waiting for transfers between devices, exchange_rows(): lax.all_to_all(x, 'expert', split_axis=0, concat_axis=0, tiled=True, axis...  23.6 us
    all_to_all x2, starting transfers between devices, exchange(): lax.all_to_all(x, 'expert', split_axis=0, concat_axis=0, tiled=True, axis...  21.1 us
    ppermute x2, starting transfers between devices, within_row(): lax.ppermute(x, 'expert', [(i, i // COLUMNS * COLUMNS + targets[i % COLUM...  13.4 us
    ppermute x3, waiting for transfers between devices, swapped(): return lax.ppermute(x, 'expert', [(i, i ^ 1) for i in range(length)])  12.2 us
    dot_general x4, matrix products, gated(): projected = jnp.dot(rows, weights, preferred_element_type=jnp.float32)  8.77 us
  transfers between devices with their start and end apart: 9, of which 7 were waited for; matrix products, arithmetic and copies ran while one was open for 6% of the time, Pallas kernels for 0%

profile of v7, /device:TPU:84, one launch (start us, length us, event | category | flops | bytes accessed | tf_op | source)
XLA Modules:
  0.0 270.4 jit_solution(11188101434334917412)
XLA Ops:
  0.0 2.6 slice_bitcast_fusion
  2.6 1.9 collective-permute-start.2
  5.9 11.5 %collective-permute-start = (bf16[32,2176]{1,0:T(8,128)(2,1)S(1)}, bf16[32,2176]{1,0:T(8,128)(2,1)S(1)}, u32[]{:S(2)}, u32[]{:S(2)}) collective-permute-start(bf16[32,2176]{1,0:T(8,128)(2,1)S(1)} %get-tuple-element.20), channel_id=1, source_target_pairs={{0,3},{1,6},{2,5},{3,0},{4,7},{5,2},{6,1},{7,4},{8,11},{9,14},{10,... | collective-permute-start | bytes 417800 | tf_op jit(solution)/shard_map/ppermute | solution.py:61
  17.4 1.9 collective-permute-start.3
  20.0 29.8 %collective-permute-done = bf16[32,2176]{1,0:T(8,128)(2,1)S(1)} collective-permute-done((bf16[32,2176]{1,0:T(8,128)(2,1)S(1)}, bf16[32,2176]{1,0:T(8,128)(2,1)S(1)}, u32[]{:S(2)}, u32[]{:S(2)}) %collective-permute-start) | collective-permute-done | bytes 139296 | tf_op jit(solution)/shard_map/ppermute | solution.py:61
  49.9 1.9 collective-permute-start.1
  52.2 6.1 %collective-permute-done.1 = bf16[2,32,2176]{2,1,0:T(8,128)(2,1)S(1)} collective-permute-done((bf16[2,32,2176]{2,1,0:T(8,128)(2,1)S(1)}, bf16[2,32,2176]{2,1,0:T(8,128)(2,1)S(1)}, u32[]{:S(2)}, u32[]{:S(2)}) %collective-permute-start.1) | collective-permute-done | bytes 278560 | tf_op jit(solution)/shard_map/ppermute | solution.py:61
  58.5 1.8 copy.232
  60.3 0.7 convert_add_fusion
  61.8 1.6 convolution_convert_fusion
  63.4 7.4 %all-to-all-start = ((bf16[8,40,2048]{2,1,0:T(8,128)(2,1)}), bf16[8,40,2048]{2,1,0:T(8,128)(2,1)S(1)}, u32[]{:S(2)}, u32[]{:S(2)}) async-start(bf16[8,40,2048]{2,1,0:T(8,128)(2,1)} %bitcast.13), calls=%async_computation | async-start | bytes 2621440 | tf_op jit(solution)/shard_map/all_to_all | solution.py:72
  70.9 1.0 slice_bitcast_fusion.7
  71.8 1.9 collective-permute-start.4
  73.8 23.6 %all-to-all-done = bf16[8,40,2048]{2,1,0:T(8,128)(2,1)S(1)} async-done(((bf16[8,40,2048]{2,1,0:T(8,128)(2,1)}), bf16[8,40,2048]{2,1,0:T(8,128)(2,1)S(1)}, u32[]{:S(2)}, u32[]{:S(2)}) %all-to-all-start) | async-done | bytes 1310752 | tf_op jit(solution)/shard_map/all_to_all | solution.py:72
  97.6 12.2 %collective-permute-done.3 = bf16[2048,768]{1,0:T(8,128)(2,1)} collective-permute-done((bf16[2048,768]{1,0:T(8,128)(2,1)}, bf16[2048,768]{1,0:T(8,128)(2,1)}, u32[]{:S(2)}, u32[]{:S(2)}) %collective-permute-start.3) | collective-permute-done | bytes 3145760 | tf_op jit(solution)/shard_map/ppermute | solution.py:77
  109.8 1.2 fusion.76
  111.0 3.2 %fusion.81 = f32[320,768]{1,0:T(8,128)S(1)} fusion(bf16[320,2048]{1,0:T(8,128)(2,1)S(1)} %pad_maximum_fusion, bf16[2048,768]{1,0:T(8,128)(2,1)} %collective-permute-done.3), kind=kOutput, calls=%fused_computation.162 | convolution fusion | flops 1006632960 | bytes 5439488 | tf_op jit(solution)/shard_map/dot_general | solution.py:82
  114.3 0.9 fusion.15
  115.9 0.9 fusion.3
  117.2 1.2 pad_maximum_fusion.1
  118.3 15.3 %all-to-all-start.1 = ((bf16[32,160,128]{2,1,0:T(8,128)(2,1)}), bf16[32,160,128]{2,1,0:T(8,128)(2,1)S(1)}, u32[]{:S(2)}, u32[]{:S(2)}) async-start(bf16[32,160,128]{2,1,0:T(8,128)(2,1)} %pad_maximum_fusion.1), calls=%async_computation.1 | async-start | bytes 2621440 | tf_op jit(solution)/shard_map/all_to_all | solution.py:56
  135.0 32.2 %all-to-all-done.1 = bf16[32,160,128]{2,1,0:T(8,128)(2,1)S(1)} async-done(((bf16[32,160,128]{2,1,0:T(8,128)(2,1)}), bf16[32,160,128]{2,1,0:T(8,128)(2,1)S(1)}, u32[]{:S(2)}, u32[]{:S(2)}) %all-to-all-start.1) | async-done | bytes 1310752 | tf_op jit(solution)/shard_map/all_to_all | solution.py:56
  168.3 1.9 collective-permute-start.5
  170.5 4.2 %collective-permute-done.5 = bf16[32,2048]{1,0:T(8,128)(2,1)S(1)} collective-permute-done((bf16[32,2048]{1,0:T(8,128)(2,1)S(1)}, bf16[32,2048]{1,0:T(8,128)(2,1)S(1)}, u32[]{:S(2)}, u32[]{:S(2)}) %collective-permute-start.5) | collective-permute-done | bytes 131104 | tf_op jit(solution)/shard_map/ppermute | solution.py:23
  175.8 41.6 %all_to_all.20 = bf16[32,160,128]{2,1,0:T(8,128)(2,1)S(1)} all-to-all(bf16[32,160,128]{2,1,0:T(8,128)(2,1)S(1)} %bitcast.173), channel_id=1, replica_groups={{0,3,4,7,8,11,12,15,16,19,20,23,24,27,28,31,32,35,36,39,40,43,44,47,48,..., dimensions={0} | all-to-all | bytes 2621440 | tf_op jit(solution)/shard_map/all_to_all | solution.py:56
  218.4 3.2 %fusion.82 = f32[320,768]{1,0:T(8,128)S(1)} fusion(bf16[320,2048]{1,0:T(8,128)(2,1)S(1)} %bitcast_dynamic-update-slice_fusion.1, bf16[2048,768]{1,0:T(8,128)(2,1)} %collective-permute-done.3), kind=kOutput, calls=%fused_computation.163 | convolution fusion | flops 1006632960 | bytes 5439488 | tf_op jit(solution)/shard_map/dot_general | solution.py:82
  221.6 1.2 fusion.74
  223.0 0.9 fusion.13
  224.5 0.9 fusion.2
  225.8 1.2 pad_maximum_fusion.2
  226.9 5.8 %all-to-all-start.3 = ((bf16[32,160,128]{2,1,0:T(8,128)(2,1)}), bf16[32,160,128]{2,1,0:T(8,128)(2,1)S(1)}, u32[]{:S(2)}, u32[]{:S(2)}) async-start(bf16[32,160,128]{2,1,0:T(8,128)(2,1)} %pad_maximum_fusion.2), calls=%async_computation.3 | async-start | bytes 2621440 | tf_op jit(solution)/shard_map/all_to_all | solution.py:56
  232.9 35.6 %all-to-all-done.3 = bf16[32,160,128]{2,1,0:T(8,128)(2,1)S(1)} async-done(((bf16[32,160,128]{2,1,0:T(8,128)(2,1)}), bf16[32,160,128]{2,1,0:T(8,128)(2,1)S(1)}, u32[]{:S(2)}, u32[]{:S(2)}) %all-to-all-start.3) | async-done | bytes 1310752 | tf_op jit(solution)/shard_map/all_to_all | solution.py:56
  (130 shorter events, 12.3 us)
Async XLA Ops:
  0.0 5.6 %copy-start.2 = (bf16[1,32,2048]{2,1,0:T(8,128)(2,1)S(1)}, bf16[1,32,2048]{2,1,0:T(8,128)(2,1)}, u32[]{:S(2)}) copy-start(bf16[1,32,2048]{2,1,0:T(8,128)(2,1)} %param.8) | copy-start | bytes 393220
  0.0 4.5 %copy-start.6 = (s32[2,1,32,4]{2,3,1,0:T(4,128)S(1)}, s32[2,1,32,4]{2,3,1,0:T(4,128)}, u32[]{:S(2)}) copy-start(s32[2,1,32,4]{2,3,1,0:T(4,128)} %param.13) | copy-start | bytes 3076
  0.0 5.7 %copy-start.4 = (f32[1,2048]{1,0:T(1,128)S(1)}, f32[1,2048]{1,0:T(1,128)}, u32[]{:S(2)}) copy-start(f32[1,2048]{1,0:T(1,128)} %param.10) | copy-start | bytes 24580
  2.6 55.8 %collective-permute-start.2 = (bf16[320,2048]{1,0:T(8,128)(2,1)}, bf16[320,2048]{1,0:T(8,128)(2,1)S(1)}, u32[]{:S(2)}, u32[]{:S(2)}) collective-permute-start(bf16[320,2048]{1,0:T(8,128)(2,1)} %slice_bitcast_fusion), channel_id=1, source_target_pairs={{0,1},{1,0},{2,3},{3,2},{4,5},{5,4},{6,7},{7,6},{8,9},{9,8},{10,11... | collective-permute-start | bytes 3932168 | tf_op jit(solution)/shard_map/ppermute | solution.py:77
  5.9 44.0 %collective-permute-start = (bf16[32,2176]{1,0:T(8,128)(2,1)S(1)}, bf16[32,2176]{1,0:T(8,128)(2,1)S(1)}, u32[]{:S(2)}, u32[]{:S(2)}) collective-permute-start(bf16[32,2176]{1,0:T(8,128)(2,1)S(1)} %get-tuple-element.20), channel_id=1, source_target_pairs={{0,3},{1,6},{2,5},{3,0},{4,7},{5,2},{6,1},{7,4},{8,11},{9,14},{10,... | collective-permute-start | bytes 417800 | tf_op jit(solution)/shard_map/ppermute | solution.py:61
  17.4 92.5 %collective-permute-start.3 = (bf16[2048,768]{1,0:T(8,128)(2,1)}, bf16[2048,768]{1,0:T(8,128)(2,1)}, u32[]{:S(2)}, u32[]{:S(2)}) collective-permute-start(bf16[2048,768]{1,0:T(8,128)(2,1)} %bitcast.200), channel_id=1, source_target_pairs={{0,1},{1,0},{2,3},{3,2},{4,5},{5,4},{6,7},{7,6},{8,9},{9,8},{10,11... | collective-permute-start | bytes 9437192 | tf_op jit(solution)/shard_map/ppermute | solution.py:77
  49.9 8.4 %collective-permute-start.1 = (bf16[2,32,2176]{2,1,0:T(8,128)(2,1)S(1)}, bf16[2,32,2176]{2,1,0:T(8,128)(2,1)S(1)}, u32[]{:S(2)}, u32[]{:S(2)}) collective-permute-start(bf16[2,32,2176]{2,1,0:T(8,128)(2,1)S(1)} %pad_maximum_fusion.5), channel_id=1, source_target_pairs={{0,7},{1,2},{2,1},{3,4},{4,3},{5,6},{6,5},{7,0},{8,15},{9,10},{10,... | collective-permute-start | bytes 835592 | tf_op jit(solution)/shard_map/ppermute | solution.py:61
  63.4 34.0 %all-to-all-start = ((bf16[8,40,2048]{2,1,0:T(8,128)(2,1)}), bf16[8,40,2048]{2,1,0:T(8,128)(2,1)S(1)}, u32[]{:S(2)}, u32[]{:S(2)}) async-start(bf16[8,40,2048]{2,1,0:T(8,128)(2,1)} %bitcast.13), calls=%async_computation | async-start | bytes 2621440 | tf_op jit(solution)/shard_map/all_to_all | solution.py:72
  71.8 43.5 %collective-permute-start.4 = (bf16[64,2048]{1,0:T(8,128)(2,1)S(1)}, bf16[64,2048]{1,0:T(8,128)(2,1)S(1)}, u32[]{:S(2)}, u32[]{:S(2)}) collective-permute-start(bf16[64,2048]{1,0:T(8,128)(2,1)S(1)} %slice_bitcast_fusion.7), channel_id=1, source_target_pairs={{0,1},{1,0},{2,3},{3,2},{4,5},{5,4},{6,7},{7,6},{8,9},{9,8},{10,11... | collective-permute-start | bytes 786440 | tf_op jit(solution)/shard_map/ppermute | solution.py:77
  97.5 12.4 %copy-start.7 = (bf16[1,1,2048,768]{3,2,1,0:T(8,128)(2,1)S(1)}, bf16[1,1,2048,768]{3,2,1,0:T(8,128)(2,1)}, u32[]{:S(2)}) copy-start(bf16[1,1,2048,768]{3,2,1,0:T(8,128)(2,1)} %param.11) | copy-start | bytes 9437188
  111.0 3.2 %copy-start = (bf16[1,1,384,2048]{3,2,1,0:T(8,128)(2,1)S(1)}, bf16[1,1,384,2048]{3,2,1,0:T(8,128)(2,1)}, u32[]{:S(2)}) copy-start(bf16[1,1,384,2048]{3,2,1,0:T(8,128)(2,1)} %param.12) | copy-start | bytes 4718596
  118.3 16.5 %copy-start.5 = (f32[2,1,32,4]{2,3,1,0:T(4,128)S(1)}, f32[2,1,32,4]{2,3,1,0:T(4,128)}, u32[]{:S(2)}) copy-start(f32[2,1,32,4]{2,3,1,0:T(4,128)} %param.14) | copy-start | bytes 3076
  118.3 48.8 %all-to-all-start.1 = ((bf16[32,160,128]{2,1,0:T(8,128)(2,1)}), bf16[32,160,128]{2,1,0:T(8,128)(2,1)S(1)}, u32[]{:S(2)}, u32[]{:S(2)}) async-start(bf16[32,160,128]{2,1,0:T(8,128)(2,1)} %pad_maximum_fusion.1), calls=%async_computation.1 | async-start | bytes 2621440 | tf_op jit(solution)/shard_map/all_to_all | solution.py:56
  167.9 6.7 %copy-start.3 = (bf16[1,32,2048]{2,1,0:T(8,128)(2,1)S(1)}, bf16[1,32,2048]{2,1,0:T(8,128)(2,1)}, u32[]{:S(2)}) copy-start(bf16[1,32,2048]{2,1,0:T(8,128)(2,1)} %param.9) | copy-start | bytes 393220
  168.3 6.3 %collective-permute-start.5 = (bf16[32,2048]{1,0:T(8,128)(2,1)S(1)}, bf16[32,2048]{1,0:T(8,128)(2,1)S(1)}, u32[]{:S(2)}, u32[]{:S(2)}) collective-permute-start(bf16[32,2048]{1,0:T(8,128)(2,1)S(1)} %fusion.11), channel_id=1, source_target_pairs={{0,64},{64,128},{128,192},{192,256},{256,320},{320,384},{384,448},... | collective-permute-start | bytes 393224 | tf_op jit(solution)/shard_map/ppermute | solution.py:23
  218.4 3.2 %copy-start.8 = (bf16[1,1,2048,768]{3,2,1,0:T(8,128)(2,1)S(1)}, bf16[1,1,2048,768]{3,2,1,0:T(8,128)(2,1)}, u32[]{:S(2)}) copy-start(bf16[1,1,2048,768]{3,2,1,0:T(8,128)(2,1)} %param.11) | copy-start | bytes 9437188
  221.6 1.4 copy-start.1
  226.9 41.6 %all-to-all-start.3 = ((bf16[32,160,128]{2,1,0:T(8,128)(2,1)}), bf16[32,160,128]{2,1,0:T(8,128)(2,1)S(1)}, u32[]{:S(2)}, u32[]{:S(2)}) async-start(bf16[32,160,128]{2,1,0:T(8,128)(2,1)} %pad_maximum_fusion.2), calls=%async_computation.3 | async-start | bytes 2621440 | tf_op jit(solution)/shard_map/all_to_all | solution.py:56
